TPU v7x, 32 devices: a whole 2x2x4 slice. The times are simulated.
32 devices in a mesh: items: 8 (over z, y), narrow: 4 (over x, core).
Axes of the slice: x: 2, y: 2, z: 4, core: 2. Of those that a mesh axis runs over, the one named last changes fastest.
Arguments:
- tokens: bfloat16 [32, 512, 768], P('items', 'narrow'), may hold values from -6 to 6
- memory: bfloat16 [32, 2048, 768], P('items', 'narrow'), may hold values from -6 to 6
- mem_count: int32 [32], P('items'), may hold values from 768 to 2048, as said below
- cotangent: bfloat16 [32, 512, 768], P('items', 'narrow'), may hold values from -6 to 6
- gain_self: float32 [768], replicated, may hold values from 0.1 to 1.9
- self_query: bfloat16 [768, 768], replicated, may hold values from -0.0546875 to 0.0546875
- self_key: bfloat16 [768, 768], replicated, may hold values from -0.21875 to 0.21875
- self_value: bfloat16 [768, 768], replicated, may hold values from -0.21875 to 0.21875
- self_out: bfloat16 [768, 768], replicated, may hold values from -0.625 to 0.625
- gain_cross: float32 [768], replicated, may hold values from 0.1 to 1.9
- cross_query: bfloat16 [768, 768], replicated, may hold values from -0.0546875 to 0.0546875
- cross_key: bfloat16 [768, 768], replicated, may hold values from -0.21875 to 0.21875
- cross_value: bfloat16 [768, 768], replicated, may hold values from -0.21875 to 0.21875
- cross_out: bfloat16 [768, 768], replicated, may hold values from -1.25 to 1.25
- gain_feed: float32 [768], replicated, may hold values from 0.1 to 1.9
- gate_weight: bfloat16 [768, 2048], replicated, may hold values from -0.21875 to 0.21875
- up_weight: bfloat16 [768, 2048], replicated, may hold values from -0.21875 to 0.21875
- down_weight: bfloat16 [2048, 768], replicated, may hold values from -0.1875 to 0.1875
Outputs:
- result: bfloat16 [32, 512, 768], P('items', 'narrow')
- tokens_grad: float32 [32, 512, 768], P('items', 'narrow')
- memory_grad: float32 [32, 2048, 768], P('items', 'narrow')
- gain_self_grad: float32 [768], replicated
- self_query_grad: float32 [768, 768], P('items', 'narrow')
- self_key_grad: float32 [768, 768], P('items', 'narrow')
- self_value_grad: float32 [768, 768], P('items', 'narrow')
- self_out_grad: float32 [768, 768], P('items', 'narrow')
- gain_cross_grad: float32 [768], replicated
- cross_query_grad: float32 [768, 768], P('items', 'narrow')
- cross_key_grad: float32 [768, 768], P('items', 'narrow')
- cross_value_grad: float32 [768, 768], P('items', 'narrow')
- cross_out_grad: float32 [768, 768], P('items', 'narrow')
- gain_feed_grad: float32 [768], replicated
- gate_weight_grad: float32 [768, 2048], P('items', 'narrow')
- up_weight_grad: float32 [768, 2048], P('items', 'narrow')
- down_weight_grad: float32 [2048, 768], P('items', 'narrow')
Inputs may be any that keep to these rules, and one draw needn't show every extreme that they name: `mem_count`: each item's count is 2048, 1024 or 768; memory rows at and past the count are padding, and every draw has items with 2048 and with 768 patches.
All inputs are finite; a program needn't handle non-finite values.
Results may differ from a plain program's by a relative error of at most 0.02555.
The roundings to bfloat16 on the way count: a program that leaves them out, or rounds other values in their place, can miss the bound.
Values may be sent and summed in bfloat16 or wider, within the bound.
No kernel may reach another device: no remote copies, remote signals or barrier semaphores. Data moves between devices by JAX's collectives and lax.ppermute only.
A program may use at most 320 MiB of HBM per device.

v0:
```python
import jax
import jax.numpy as jnp
from jax import lax
from jax.sharding import PartitionSpec as P

H = 12
HD = 64


eps = 1e-06
neg_big = -1e30
gelu_scale = 0.7978845608028654


def rms_scale(hidden_rows, gain_vector):
    inverse = lax.rsqrt(jnp.mean(hidden_rows * hidden_rows, axis=-1, keepdims=True) + eps)
    return hidden_rows * inverse * gain_vector


def gelu_tanh(inputs):
    return (
        0.5 * inputs * (1.0 + jnp.tanh(gelu_scale * (inputs + 0.044715 * inputs * inputs * inputs)))
    )


def gated_unit(gate_pre, up_pre):
    return gelu_tanh(gate_pre) * up_pre


def project(left_side, right_side):
    return jnp.dot(left_side, right_side, preferred_element_type=jnp.float32)


def outer_rows(left_side, right_side):
    return lax.dot_general(
        left_side, right_side, (((0,), (0,)), ((), ())), preferred_element_type=jnp.float32
    )


def back_project(grad_rows, weights):
    return lax.dot_general(
        grad_rows, weights, (((1,), (1,)), ((), ())), preferred_element_type=jnp.float32
    )


def norm_back(hidden_rows, gain_vector, grad_normed):
    unused, pullback = jax.vjp(rms_scale, hidden_rows, gain_vector)
    return pullback(grad_normed)


def attend_forward(queries, keys_in, values_in, allowed):
    scores = jnp.einsum("bqhd,bkhd->bhqk", queries, keys_in, preferred_element_type=jnp.float32)
    scores = jnp.where(allowed, scores, neg_big)
    row_peak = jnp.max(scores, axis=-1, keepdims=True)
    exp_scores = jnp.exp(scores - row_peak)
    row_total = jnp.sum(exp_scores, axis=-1, keepdims=True)
    prob_low = (exp_scores / row_total).astype(jnp.bfloat16)
    mixed_heads = jnp.einsum(
        "bhqk,bkhd->bqhd", prob_low, values_in, preferred_element_type=jnp.float32
    )
    return (mixed_heads.astype(jnp.bfloat16), row_peak + jnp.log(row_total))


def attend_backward(queries, keys_in, values_in, allowed, log_total, grad_mixed):
    scores = jnp.einsum("bqhd,bkhd->bhqk", queries, keys_in, preferred_element_type=jnp.float32)
    scores = jnp.where(allowed, scores, neg_big)
    probs_full = jnp.exp(scores - log_total)
    grad_probs = jnp.einsum(
        "bqhd,bkhd->bhqk", grad_mixed, values_in, preferred_element_type=jnp.float32
    )
    centre = jnp.sum(probs_full * grad_probs, axis=-1, keepdims=True)
    grad_scores = (probs_full * (grad_probs - centre)).astype(jnp.bfloat16)
    grad_queries = jnp.einsum(
        "bhqk,bkhd->bqhd", grad_scores, keys_in, preferred_element_type=jnp.float32
    )
    grad_keys = jnp.einsum(
        "bhqk,bqhd->bkhd", grad_scores, queries, preferred_element_type=jnp.float32
    )
    grad_values = jnp.einsum(
        "bhqk,bqhd->bkhd",
        probs_full.astype(jnp.bfloat16),
        grad_mixed,
        preferred_element_type=jnp.float32,
    )
    return (grad_queries, grad_keys, grad_values)


def cross_forward(packed):
    mixed_heads, log_total = attend_forward(
        packed[0][None], packed[1][None], packed[2][None], packed[3][None, None, None, :]
    )
    return (mixed_heads[0], log_total[0])


def cross_backward(packed):
    grad_triple = attend_backward(
        packed[0][None],
        packed[1][None],
        packed[2][None],
        packed[3][None, None, None, :],
        packed[4][None],
        packed[5][None],
    )
    return (grad_triple[0][0], grad_triple[1][0], grad_triple[2][0])


def split_heads(flat_rows):
    return flat_rows.reshape(flat_rows.shape[0], -1, H, HD)


def block_grid(piece, row_parts, col_parts):
    rows_all, cols_all = piece.shape
    grid = piece.reshape(row_parts, rows_all // row_parts, col_parts, cols_all // col_parts)
    return grid.transpose(0, 2, 1, 3)


def body(
    tokens,
    memory,
    mem_count,
    cotangent,
    gain_self,
    self_query,
    self_key,
    self_value,
    self_out,
    gain_cross,
    cross_query,
    cross_key,
    cross_value,
    cross_out,
    gain_feed,
    gate_weight,
    up_weight,
    down_weight,
):
    batch_size, local_tok, model_width = tokens.shape
    local_mem = memory.shape[1]
    narrow_count = lax.axis_size("narrow")
    full_tok = local_tok * narrow_count
    full_mem = local_mem * narrow_count
    token_rows = tokens.astype(jnp.float32).reshape(-1, model_width)
    normed_one = rms_scale(token_rows, gain_self).astype(jnp.bfloat16)
    query_one = (
        project(normed_one, self_query)
        .astype(jnp.bfloat16)
        .reshape(batch_size, local_tok, model_width)
    )
    key_one = (
        project(normed_one, self_key)
        .astype(jnp.bfloat16)
        .reshape(batch_size, local_tok, model_width)
    )
    value_one = (
        project(normed_one, self_value)
        .astype(jnp.bfloat16)
        .reshape(batch_size, local_tok, model_width)
    )
    keys_all, values_all = (
        lax.all_gather(key_one, "narrow", axis=1, tiled=True),
        lax.all_gather(value_one, "narrow", axis=1, tiled=True),
    )
    shard_place = lax.axis_index("narrow")
    query_pos = shard_place * local_tok + jnp.arange(local_tok, dtype=jnp.int32)
    causal = (jnp.arange(full_tok, dtype=jnp.int32)[None, :] <= query_pos[:, None])[None, None]
    attended_one, total_one = attend_forward(
        split_heads(query_one), split_heads(keys_all), split_heads(values_all), causal
    )
    attended_flat = attended_one.reshape(-1, model_width)
    hidden_one = token_rows + project(attended_flat, self_out)
    normed_two = rms_scale(hidden_one, gain_cross).astype(jnp.bfloat16)
    query_two = (
        project(normed_two, cross_query)
        .astype(jnp.bfloat16)
        .reshape(batch_size, local_tok, model_width)
    )
    memory_rows = memory.reshape(-1, model_width)
    memory_key = (
        project(memory_rows, cross_key)
        .astype(jnp.bfloat16)
        .reshape(batch_size, local_mem, model_width)
    )
    memory_value = (
        project(memory_rows, cross_value)
        .astype(jnp.bfloat16)
        .reshape(batch_size, local_mem, model_width)
    )
    memory_keys_all, memory_values_all = (
        lax.all_gather(memory_key, "narrow", axis=1, tiled=True),
        lax.all_gather(memory_value, "narrow", axis=1, tiled=True),
    )
    patch_live = jnp.arange(full_mem, dtype=jnp.int32)[None, :] < mem_count[:, None]
    crossed, total_two = lax.map(
        cross_forward,
        (
            split_heads(query_two),
            split_heads(memory_keys_all),
            split_heads(memory_values_all),
            patch_live,
        ),
    )
    crossed_flat = crossed.reshape(-1, model_width)
    hidden_two = hidden_one + project(crossed_flat, cross_out)
    normed_three = rms_scale(hidden_two, gain_feed).astype(jnp.bfloat16)
    gate_pre = project(normed_three, gate_weight)
    up_pre = project(normed_three, up_weight)
    mixed_full, mix_back = jax.vjp(gated_unit, gate_pre, up_pre)
    mixed = mixed_full.astype(jnp.bfloat16)
    result = (hidden_two + project(mixed, down_weight)).astype(jnp.bfloat16).reshape(tokens.shape)
    grad_rows = cotangent.astype(jnp.float32).reshape(-1, model_width)
    grad_branch = grad_rows.astype(jnp.bfloat16)
    grad_down = outer_rows(mixed, grad_branch)
    grad_gate, grad_up = mix_back(back_project(grad_branch, down_weight))
    grad_gate = grad_gate.astype(jnp.bfloat16)
    grad_up = grad_up.astype(jnp.bfloat16)
    grad_gate_weight = outer_rows(normed_three, grad_gate)
    grad_up_weight = outer_rows(normed_three, grad_up)
    grad_normed_three = back_project(grad_gate, gate_weight) + back_project(grad_up, up_weight)
    grad_norm_two, grad_gain_feed = norm_back(hidden_two, gain_feed, grad_normed_three)
    grad_hidden_two = grad_rows + grad_norm_two
    branch_two_grad = grad_hidden_two.astype(jnp.bfloat16)
    grad_cross_out = outer_rows(crossed_flat, branch_two_grad)
    grad_crossed = (
        back_project(branch_two_grad, cross_out)
        .astype(jnp.bfloat16)
        .reshape(batch_size, local_tok, H, HD)
    )
    grad_query_two, grad_memory_keys, grad_memory_values = lax.map(
        cross_backward,
        (
            split_heads(query_two),
            split_heads(memory_keys_all),
            split_heads(memory_values_all),
            patch_live,
            total_two,
            grad_crossed,
        ),
    )
    memory_keys_grad, memory_values_grad = (
        lax.psum_scatter(
            grad_memory_keys.reshape(batch_size, full_mem, model_width).astype(jnp.bfloat16),
            "narrow",
            scatter_dimension=1,
            tiled=True,
        ).astype(jnp.float32),
        lax.psum_scatter(
            grad_memory_values.reshape(batch_size, full_mem, model_width).astype(jnp.bfloat16),
            "narrow",
            scatter_dimension=1,
            tiled=True,
        ).astype(jnp.float32),
    )
    memory_keys_grad = memory_keys_grad.astype(jnp.bfloat16).reshape(-1, model_width)
    memory_values_grad = memory_values_grad.astype(jnp.bfloat16).reshape(-1, model_width)
    grad_cross_key = outer_rows(memory_rows, memory_keys_grad)
    grad_cross_value = outer_rows(memory_rows, memory_values_grad)
    memory_grad = (
        back_project(memory_keys_grad, cross_key) + back_project(memory_values_grad, cross_value)
    ).reshape(memory.shape)
    grad_query_two = grad_query_two.astype(jnp.bfloat16).reshape(-1, model_width)
    grad_cross_query = outer_rows(normed_two, grad_query_two)
    grad_norm_one, grad_gain_cross = norm_back(
        hidden_one, gain_cross, back_project(grad_query_two, cross_query)
    )
    grad_hidden_one = grad_hidden_two + grad_norm_one
    branch_one_grad = grad_hidden_one.astype(jnp.bfloat16)
    grad_self_out = outer_rows(attended_flat, branch_one_grad)
    grad_attended = (
        back_project(branch_one_grad, self_out)
        .astype(jnp.bfloat16)
        .reshape(batch_size, local_tok, H, HD)
    )
    grad_query_one, grad_keys_one, grad_values_one = attend_backward(
        split_heads(query_one),
        split_heads(keys_all),
        split_heads(values_all),
        causal,
        total_one,
        grad_attended,
    )
    key_one_grad, value_one_grad = (
        lax.psum_scatter(
            grad_keys_one.reshape(batch_size, full_tok, model_width).astype(jnp.bfloat16),
            "narrow",
            scatter_dimension=1,
            tiled=True,
        ).astype(jnp.float32),
        lax.psum_scatter(
            grad_values_one.reshape(batch_size, full_tok, model_width).astype(jnp.bfloat16),
            "narrow",
            scatter_dimension=1,
            tiled=True,
        ).astype(jnp.float32),
    )
    key_one_grad = key_one_grad.astype(jnp.bfloat16).reshape(-1, model_width)
    value_one_grad = value_one_grad.astype(jnp.bfloat16).reshape(-1, model_width)
    grad_query_one = grad_query_one.astype(jnp.bfloat16).reshape(-1, model_width)
    grad_self_query = outer_rows(normed_one, grad_query_one)
    grad_self_key = outer_rows(normed_one, key_one_grad)
    grad_self_value = outer_rows(normed_one, value_one_grad)
    grad_normed_one = (
        back_project(grad_query_one, self_query)
        + back_project(key_one_grad, self_key)
        + back_project(value_one_grad, self_value)
    )
    grad_norm_zero, grad_gain_self = norm_back(token_rows, gain_self, grad_normed_one)
    tokens_grad = (grad_hidden_one + grad_norm_zero).reshape(tokens.shape)
    gains_summed = lax.psum((grad_gain_self, grad_gain_cross, grad_gain_feed), ("items", "narrow"))
    spread = lax.axis_size("items")
    local_parts = [
        grad_self_query,
        grad_self_key,
        grad_self_value,
        grad_self_out,
        grad_cross_query,
        grad_cross_key,
        grad_cross_value,
        grad_cross_out,
        grad_gate_weight,
        grad_up_weight,
        grad_down,
    ]
    grids = [block_grid(piece, spread, narrow_count) for piece in local_parts]
    flat_grids = [piece.reshape((spread * narrow_count,) + piece.shape[2:]) for piece in grids]
    joint_sums = (
        lax.psum_scatter(flat_grids[0], ("items", "narrow"), scatter_dimension=0, tiled=True),
        lax.psum_scatter(flat_grids[1], ("items", "narrow"), scatter_dimension=0, tiled=True),
        lax.psum_scatter(flat_grids[2], ("items", "narrow"), scatter_dimension=0, tiled=True),
        lax.psum_scatter(flat_grids[3], ("items", "narrow"), scatter_dimension=0, tiled=True),
        lax.psum_scatter(flat_grids[4], ("items", "narrow"), scatter_dimension=0, tiled=True),
        lax.psum_scatter(flat_grids[5], ("items", "narrow"), scatter_dimension=0, tiled=True),
        lax.psum_scatter(flat_grids[6], ("items", "narrow"), scatter_dimension=0, tiled=True),
        lax.psum_scatter(flat_grids[7], ("items", "narrow"), scatter_dimension=0, tiled=True),
        lax.psum_scatter(flat_grids[8], ("items", "narrow"), scatter_dimension=0, tiled=True),
        lax.psum_scatter(flat_grids[9], ("items", "narrow"), scatter_dimension=0, tiled=True),
        lax.psum_scatter(flat_grids[10], ("items", "narrow"), scatter_dimension=0, tiled=True),
    )
    summed = [piece[0] for piece in joint_sums]
    return (
        result,
        tokens_grad,
        memory_grad,
        gains_summed[0],
        summed[0],
        summed[1],
        summed[2],
        summed[3],
        gains_summed[1],
        summed[4],
        summed[5],
        summed[6],
        summed[7],
        gains_summed[2],
        summed[8],
        summed[9],
        summed[10],
    )


def solution(mesh):
    in_specs = (
        P("items", "narrow", None),
        P("items", "narrow", None),
        P("items"),
        P("items", "narrow", None),
        P(),
        P(),
        P(),
        P(),
        P(),
        P(),
        P(),
        P(),
        P(),
        P(),
        P(),
        P(),
        P(),
        P(),
    )
    out_specs = (
        P("items", "narrow", None),
        P("items", "narrow", None),
        P("items", "narrow", None),
        P(),
        P("items", "narrow"),
        P("items", "narrow"),
        P("items", "narrow"),
        P("items", "narrow"),
        P(),
        P("items", "narrow"),
        P("items", "narrow"),
        P("items", "narrow"),
        P("items", "narrow"),
        P(),
        P("items", "narrow"),
        P("items", "narrow"),
        P("items", "narrow"),
    )
    return jax.shard_map(body, mesh=mesh, in_specs=in_specs, out_specs=out_specs, check_vma=False)
```

profile of v0, /device:TPU:0, one launch (start us, length us, event | category | flops | bytes accessed | tf_op | source)
XLA Modules:
  0.0 2032.0 jit_solution(1833925325666030729)
XLA Ops:
  17.9 5.3 convolution_convert_fusion.1
  23.3 5.3 convolution_convert_fusion
  37.2 8.8 all-gather.5.cloned.1.call-done
  46.0 4.6 copy.95
  50.6 26.1 %all-gather.7.cloned.1.call-done = bf16[4,512,768]{2,1,0:T(8,128)(2,1)} async-done(((bf16[4,128,768]{2,1,0:T(8,128)(2,1)}), bf16[4,512,768]{2,1,0:T(8,128)(2,1)}) %all-gather.7.cloned.1.call-update) | async-done | bytes 3145744 | tf_op jit(solution)/shard_map/all_gather | solution.py:160
  76.7 4.7 copy.97
  92.8 4.6 fusion.93
  109.5 50.9 %all-gather.9.cloned.1.call-done = bf16[4,2048,768]{2,1,0:T(8,128)(2,1)} async-done(((bf16[4,512,768]{2,1,0:T(8,128)(2,1)}), bf16[4,2048,768]{2,1,0:T(8,128)(2,1)}) %all-gather.9.cloned.1.call-update) | async-done | bytes 12582928 | tf_op jit(solution)/shard_map/all_gather | solution.py:190
  160.4 16.6 copy.100
  177.0 67.0 %all-gather.11.cloned.1.call-done = bf16[4,2048,768]{2,1,0:T(8,128)(2,1)} async-done(((bf16[4,512,768]{2,1,0:T(8,128)(2,1)}), bf16[4,2048,768]{2,1,0:T(8,128)(2,1)}) %all-gather.11.cloned.1.call-update) | async-done | bytes 12582928 | tf_op jit(solution)/shard_map/all_gather | solution.py:189
  244.0 16.8 copy.102
  260.8 47.7 %while.26 = (s32[]{:T(128)}, bf16[4,128,12,64]{1,3,2,0:T(8,128)(2,1)}, f32[4,12,128,1]{2,1,3,0:T(8,128)S(1)}, bf16[4,2048,12,64]{1,3,2,0:T(8,128)(2,1)}, pred[4,...) while((s32[]{:T(128)}, ...), condition=%wide.region_7.8_spmd, body=%wide.region_4.7_spmd.sunk | while | flops 833714688 | bytes 44501092 | solution.py:193
  267.6 5.4 fusion.209
  279.4 5.4 fusion.209
  291.2 5.4 fusion.209
  303.1 5.4 fusion.209
  320.0 16.6 multiply_convert_fusion.2
  352.6 136.5 %while.27 = (s32[]{:T(128)}, bf16[4,128,12,64]{1,3,2,0:T(8,128)(2,1)}, bf16[4,2048,12,64]{1,3,2,0:T(8,128)(2,1)}, bf16[4,2048,12,64]{1,3,2,0:T(8,128)(2,1)}, bf1...) while((s32[]{:T(128)}, ...), condition=%wide.region_12.13_spmd, body=%wide.region_10.12_spmd.sunk | while | flops 2051013120 | bytes 123921592 | solution.py:228
  356.5 10.3 multiply_reduce_fusion.9
  366.7 6.5 multiply_convert_fusion.11
  381.4 5.1 bitcast_dynamic-update-slice_fusion.8
  390.5 10.2 multiply_reduce_fusion.9
  400.7 6.5 multiply_convert_fusion.11
  415.5 5.1 bitcast_dynamic-update-slice_fusion.8
  424.5 10.3 multiply_reduce_fusion.9
  434.7 6.5 multiply_convert_fusion.11
  449.6 5.1 bitcast_dynamic-update-slice_fusion.8
  458.6 10.2 multiply_reduce_fusion.9
  468.8 6.5 multiply_convert_fusion.11
  483.6 5.1 bitcast_dynamic-update-slice_fusion.8
  503.5 8.3 multiply_reduce_fusion.1
  511.8 6.7 multiply_convert_fusion.1
  522.1 4.7 copy.113
  526.9 9.1 fusion.78
  536.0 4.7 copy.115
  544.8 6.1 fusion.92
  581.4 6.4 fusion.125
  587.8 8.4 reshape.429
  596.3 7.4 copy.126
  603.9 6.4 fusion.126
  610.3 9.0 reshape.431
  619.3 8.7 copy.127
  634.4 6.3 fusion.127
  653.7 53.6 %reduce-scatter.20.cloned.1.call-done = bf16[4,512,768]{1,2,0:T(8,128)(2,1)} async-done(((bf16[4,2048,768]{1,2,0:T(8,128)(2,1)}), bf16[4,512,768]{1,2,0:T(8,128)(2,1)}) %reduce-scatter.20.cloned.1.call-update) | async-done | bytes 3145744 | tf_op jit(solution)/shard_map/reduce_scatter | solution.py:240
  707.3 5.9 convolution_bitcast_fusion.1
  722.4 86.5 %reduce-scatter.22.cloned.1.call-done = bf16[4,512,768]{1,2,0:T(8,128)(2,1)} async-done(((bf16[4,2048,768]{1,2,0:T(8,128)(2,1)}), bf16[4,512,768]{1,2,0:T(8,128)(2,1)}) %reduce-scatter.22.cloned.1.call-update) | async-done | bytes 3145744 | tf_op jit(solution)/shard_map/reduce_scatter | solution.py:246
  808.9 5.9 convolution_bitcast_fusion
  823.1 8.7 add_convert_fusion
  836.2 40.4 %all-reduce = (f32[768]{0:T(1024)}, f32[768]{0:T(1024)}, f32[768]{0:T(1024)}) all-reduce(f32[768]{0:T(1024)S(1)} %get-tuple-element.169, f32[768]{0:T(1024)S(1)} %get-tuple-element.167, f32[768]{0:T(1024)S(1)} %copy-done.46), channel_id=1, replica_groups=mesh['items'=8,'narrow'=4] {'items','narrow'}, use_global_device_ids=true, to_apply=%region_21.22 | all-reduce | flops 2304 | bytes 18432 | tf_op jit(solution)/shard_map/psum | solution.py:308
  880.4 4.6 copy.116
  885.0 4.7 copy.117
  889.7 5.1 fusion.118
  894.8 4.5 convolution_add_fusion
  899.4 17.4 reduce-scatter.24.cloned.1.call-done
  916.8 106.4 %reduce-scatter.30.cloned.1.call-done = f32[1,96,192]{2,1,0:T(8,128)} async-done(((f32[32,96,192]{2,1,0:T(8,128)}), f32[1,96,192]{2,1,0:T(8,128)}) %reduce-scatter.30.cloned.1.call-update) | async-done | bytes 73744 | tf_op jit(solution)/shard_map/reduce_scatter | solution.py:329
  1023.2 106.5 %reduce-scatter.32.cloned.1.call-done = f32[1,96,192]{2,1,0:T(8,128)} async-done(((f32[32,96,192]{2,1,0:T(8,128)}), f32[1,96,192]{2,1,0:T(8,128)}) %reduce-scatter.32.cloned.1.call-update) | async-done | bytes 73744 | tf_op jit(solution)/shard_map/reduce_scatter | solution.py:330
  1129.7 106.4 %reduce-scatter.38.cloned.1.call-done = f32[1,96,192]{2,1,0:T(8,128)} async-done(((f32[32,96,192]{2,1,0:T(8,128)}), f32[1,96,192]{2,1,0:T(8,128)}) %reduce-scatter.38.cloned.1.call-update) | async-done | bytes 73744 | tf_op jit(solution)/shard_map/reduce_scatter | solution.py:333
  1236.1 119.6 %reduce-scatter.40.cloned.1.call-done = f32[1,96,512]{2,1,0:T(8,128)} async-done(((f32[32,96,512]{2,1,0:T(8,128)}), f32[1,96,512]{2,1,0:T(8,128)}) %reduce-scatter.40.cloned.1.call-update) | async-done | bytes 196624 | tf_op jit(solution)/shard_map/reduce_scatter | solution.py:334
  1355.7 120.5 %reduce-scatter.42.cloned.1.call-done = f32[1,96,512]{2,1,0:T(8,128)} async-done(((f32[32,96,512]{2,1,0:T(8,128)}), f32[1,96,512]{2,1,0:T(8,128)}) %reduce-scatter.42.cloned.1.call-update) | async-done | bytes 196624 | tf_op jit(solution)/shard_map/reduce_scatter | solution.py:335
  1476.2 119.6 %reduce-scatter.44.cloned.1.call-done = f32[1,256,192]{1,2,0:T(8,128)} async-done(((f32[32,256,192]{1,2,0:T(8,128)}), f32[1,256,192]{1,2,0:T(8,128)}) %reduce-scatter.44.cloned.1.call-update) | async-done | bytes 196624 | tf_op jit(solution)/shard_map/reduce_scatter | solution.py:336
  1595.8 107.5 %reduce-scatter.26.cloned.1.call-done = f32[1,96,192]{2,1,0:T(8,128)} async-done(((f32[32,96,192]{2,1,0:T(8,128)}), f32[1,96,192]{2,1,0:T(8,128)}) %reduce-scatter.26.cloned.1.call-update) | async-done | bytes 73744 | tf_op jit(solution)/shard_map/reduce_scatter | solution.py:327
  1703.3 107.3 %reduce-scatter.28.cloned.1.call-done = f32[1,96,192]{2,1,0:T(8,128)} async-done(((f32[32,96,192]{2,1,0:T(8,128)}), f32[1,96,192]{2,1,0:T(8,128)}) %reduce-scatter.28.cloned.1.call-update) | async-done | bytes 73744 | tf_op jit(solution)/shard_map/reduce_scatter | solution.py:328
  1810.6 107.3 %reduce-scatter.34.cloned.1.call-done = f32[1,96,192]{2,1,0:T(8,128)} async-done(((f32[32,96,192]{2,1,0:T(8,128)}), f32[1,96,192]{2,1,0:T(8,128)}) %reduce-scatter.34.cloned.1.call-update) | async-done | bytes 73744 | tf_op jit(solution)/shard_map/reduce_scatter | solution.py:331
  1917.9 107.4 %reduce-scatter.36.cloned.1.call-done = f32[1,96,192]{2,1,0:T(8,128)} async-done(((f32[32,96,192]{2,1,0:T(8,128)}), f32[1,96,192]{2,1,0:T(8,128)}) %reduce-scatter.36.cloned.1.call-update) | async-done | bytes 73744 | tf_op jit(solution)/shard_map/reduce_scatter | solution.py:332
  (282 shorter events, 241.7 us)
Async XLA Ops:
  7.2 10.7 copy-start
  7.2 38.8 %all-gather.5.cloned.1.call-start = ((), (), s32[]{:S(2)}) async-start(), calls=%async_computation.15 | async-start | bytes 3932160 | tf_op jit(solution)/shard_map/all_gather | solution.py:161
  9.3 5.3 copy-start.35
  14.6 62.1 %all-gather.7.cloned.1.call-start = ((), (), s32[]{:S(2)}) async-start(), calls=%async_computation.16 | async-start | bytes 3932160 | tf_op jit(solution)/shard_map/all_gather | solution.py:160
  17.9 142.6 %all-gather.9.cloned.1.call-start = ((), (), s32[]{:S(2)}) async-start(), calls=%async_computation.17 | async-start | bytes 15728640 | tf_op jit(solution)/shard_map/all_gather | solution.py:190
  23.2 220.8 %all-gather.11.cloned.1.call-start = ((), (), s32[]{:S(2)}) async-start(), calls=%async_computation.18 | async-start | bytes 15728640 | tf_op jit(solution)/shard_map/all_gather | solution.py:189
  28.6 612.1 %reduce-scatter.16.cloned.1.call-start = ((), (), s32[]{:S(2)}) async-start(), calls=%async_computation.19 | async-start | bytes 3932160 | tf_op jit(solution)/shard_map/reduce_scatter | solution.py:282
  29.0 8.1 copy-start.47
  37.1 51.9 %copy-start.16 = (pred[128,512]{1,0:T(8,128)(4,1)}, pred[128,512]{1,0:T(8,128)(4,1)S(1)}, u32[]{:S(2)}) copy-start(pred[128,512]{1,0:T(8,128)(4,1)S(1)} %iota_compare_fusion) | copy-start | bytes 196612
  85.6 7.2 copy-start.1
  85.6 7.2 copy-start.3
  92.8 5.2 copy-start.6
  92.8 5.2 copy-start.52
  98.0 2.1 copy-start.44
  308.5 4.9 copy-start.39
  310.2 3.1 copy-start.10
  310.2 3.3 copy-start.48
  313.3 28.0 %copy-start.4 = (f32[512,768]{1,0:T(8,128)}, f32[512,768]{1,0:T(8,128)S(1)}, u32[]{:S(2)}) copy-start(f32[512,768]{1,0:T(8,128)S(1)} %get-tuple-element.224) | copy-start | bytes 4718596
  313.5 2.5 copy-start.49
  316.0 3.9 copy-start.57
  316.0 3.9 copy-start.18
  316.0 4.0 copy-start.50
  319.9 16.7 copy-start.58
  341.3 2.6 copy-start.28
  352.6 138.3 %copy-start.41 = (f32[512]{0:T(512)S(1)}, f32[512]{0:T(512)}, u32[]{:S(2)}) copy-start(f32[512]{0:T(512)} %copy-done.40) | copy-start | bytes 6148
  352.6 138.3 %copy-start.45 = (f32[768]{0:T(1024)S(1)}, f32[768]{0:T(1024)}, u32[]{:S(2)}) copy-start(f32[768]{0:T(1024)} %param.31) | copy-start | bytes 9220
  366.7 6.5 copy-start.31
  377.6 3.8 copy-start.32
  400.7 6.5 copy-start.31
  411.6 3.9 copy-start.32
  434.7 6.5 copy-start.31
  445.6 3.9 copy-start.32
  468.8 6.5 copy-start.31
  479.7 3.8 copy-start.32
  490.8 3.2 copy-start.24
  490.8 3.2 copy-start.43
  490.8 3.2 copy-start.13
  490.9 3.2 copy-start.15
  494.1 2.9 copy-start.53
  497.0 6.5 copy-start.17
  497.0 6.5 copy-start.33
  511.8 6.7 copy-start.8
  518.5 3.7 copy-start.2
  526.9 120.3 %reduce-scatter.18.cloned.1.call-start = ((), (), s32[]{:S(2)}) async-start(), calls=%async_computation.20 | async-start | bytes 3932160 | tf_op jit(solution)/shard_map/reduce_scatter | solution.py:288
  540.7 166.5 %reduce-scatter.20.cloned.1.call-start = ((), (), s32[]{:S(2)}) async-start(), calls=%async_computation.21 | async-start | bytes 15728640 | tf_op jit(solution)/shard_map/reduce_scatter | solution.py:240
  541.5 267.5 %reduce-scatter.22.cloned.1.call-start = ((), (), s32[]{:S(2)}) async-start(), calls=%async_computation.22 | async-start | bytes 15728640 | tf_op jit(solution)/shard_map/reduce_scatter | solution.py:246
  542.2 374.6 %reduce-scatter.24.cloned.1.call-start = ((), (), s32[]{:S(2)}) async-start(), calls=%async_computation.23 | async-start | bytes 3244032 | tf_op jit(solution)/shard_map/reduce_scatter | solution.py:326
  555.4 467.8 %reduce-scatter.30.cloned.1.call-start = ((), (), s32[]{:S(2)}) async-start(), calls=%async_computation.26 | async-start | bytes 3244032 | tf_op jit(solution)/shard_map/reduce_scatter | solution.py:329
  563.9 565.8 %reduce-scatter.32.cloned.1.call-start = ((), (), s32[]{:S(2)}) async-start(), calls=%async_computation.27 | async-start | bytes 3244032 | tf_op jit(solution)/shard_map/reduce_scatter | solution.py:330
  572.5 663.6 %reduce-scatter.38.cloned.1.call-start = ((), (), s32[]{:S(2)}) async-start(), calls=%async_computation.30 | async-start | bytes 3244032 | tf_op jit(solution)/shard_map/reduce_scatter | solution.py:333
  581.4 774.3 %reduce-scatter.40.cloned.1.call-start = ((), (), s32[]{:S(2)}) async-start(), calls=%async_computation.31 | async-start | bytes 6488064 | tf_op jit(solution)/shard_map/reduce_scatter | solution.py:334
  603.7 872.6 %reduce-scatter.42.cloned.1.call-start = ((), (), s32[]{:S(2)}) async-start(), calls=%async_computation.32 | async-start | bytes 6488064 | tf_op jit(solution)/shard_map/reduce_scatter | solution.py:335
  628.0 967.8 %reduce-scatter.44.cloned.1.call-start = ((), (), s32[]{:S(2)}) async-start(), calls=%async_computation.33 | async-start | bytes 6488064 | tf_op jit(solution)/shard_map/reduce_scatter | solution.py:336
  640.7 1062.6 %reduce-scatter.26.cloned.1.call-start = ((), (), s32[]{:S(2)}) async-start(), calls=%async_computation.24 | async-start | bytes 3244032 | tf_op jit(solution)/shard_map/reduce_scatter | solution.py:327
  647.2 1163.5 %reduce-scatter.28.cloned.1.call-start = ((), (), s32[]{:S(2)}) async-start(), calls=%async_computation.25 | async-start | bytes 3244032 | tf_op jit(solution)/shard_map/reduce_scatter | solution.py:328
  653.6 1264.3 %reduce-scatter.34.cloned.1.call-start = ((), (), s32[]{:S(2)}) async-start(), calls=%async_computation.28 | async-start | bytes 3244032 | tf_op jit(solution)/shard_map/reduce_scatter | solution.py:331
  722.1 1303.2 %reduce-scatter.36.cloned.1.call-start = ((), (), s32[]{:S(2)}) async-start(), calls=%async_computation.29 | async-start | bytes 3244032 | tf_op jit(solution)/shard_map/reduce_scatter | solution.py:332
  823.1 8.7 copy-start.23
  823.1 8.7 copy-start.54
  823.1 9.6 copy-start.55
  833.9 2.3 copy-start.46
  833.9 42.7 %copy-start.38 = (f32[4,128]{1,0:T(4,128)S(1)}, f32[4,128]{1,0:T(4,128)}, u32[]{:S(2)}) copy-start(f32[4,128]{1,0:T(4,128)} %copy-done.37) | copy-start | bytes 6148
  889.7 5.1 copy-start.19
  889.7 5.1 copy-start.56
  (20 other events, 28.8 us)
Sparse Core Ops, SparseCore 0:
  14.7 31.2 all-gather.4
  48.1 28.5 all-gather.6
  78.3 82.0 all-gather.8
  161.8 82.0 all-gather.10
  527.0 37.9 reduce-scatter.15
  567.6 37.9 reduce-scatter.17
  608.2 99.0 reduce-scatter.19
  709.9 99.0 reduce-scatter.21
  814.9 101.8 reduce-scatter.23
  922.7 100.4 reduce-scatter.29
  1029.2 100.4 reduce-scatter.31
  1135.6 100.4 reduce-scatter.37
  1242.3 113.3 reduce-scatter.39
  1362.7 113.4 reduce-scatter.41
  1482.3 113.5 reduce-scatter.43
  1602.6 100.7 reduce-scatter.25
  1710.1 100.5 reduce-scatter.27
  1817.4 100.4 reduce-scatter.33
  1924.8 100.5 reduce-scatter.35
where the time goes:
time: 2040 us; the launch traced here: 2030 us
  waiting for transfers between devices  1420 us (70%)
  matrix products  317 us (16%)
  local copies, waits for them, and re-layouts  179 us (9%)
  other arithmetic  56.7 us (3%)
  blocking collectives  40.4 us (2%)
    reduce_scatter x1, waiting for transfers between devices, body(): lax.psum_scatter(flat_grids[9], ('items', 'narrow'), scatter_dimension=0,...  121 us
    reduce_scatter x1, waiting for transfers between devices, body(): lax.psum_scatter(flat_grids[10], ('items', 'narrow'), scatter_dimension=0...  120 us
    reduce_scatter x1, waiting for transfers between devices, body(): lax.psum_scatter(flat_grids[8], ('items', 'narrow'), scatter_dimension=0,...  120 us
    reduce_scatter x1, waiting for transfers between devices, body(): lax.psum_scatter(flat_grids[1], ('items', 'narrow'), scatter_dimension=0,...  107 us
    reduce_scatter x1, waiting for transfers between devices, body(): lax.psum_scatter(flat_grids[6], ('items', 'narrow'), scatter_dimension=0,...  107 us
    reduce_scatter x1, waiting for transfers between devices, body(): lax.psum_scatter(flat_grids[2], ('items', 'narrow'), scatter_dimension=0,...  107 us
    reduce_scatter x1, waiting for transfers between devices, body(): lax.psum_scatter(flat_grids[5], ('items', 'narrow'), scatter_dimension=0,...  107 us
    reduce_scatter x1, waiting for transfers between devices, body(): lax.psum_scatter(flat_grids[4], ('items', 'narrow'), scatter_dimension=0,...  107 us
  transfers between devices with their start and end apart: 19, of which 17 were waited for; matrix products, arithmetic and copies ran while one was open for 13% of the time, Pallas kernels for 0%

commit v1 on v0

v1 whole, which is shorter than its diff:
```python
import jax
import jax.numpy as jnp
from jax import lax
from jax.sharding import PartitionSpec as P

H = 12
HD = 64


eps = 1e-06
neg_big = -1e30
gelu_scale = 0.7978845608028654


def rms_scale(hidden_rows, gain_vector):
    inverse = lax.rsqrt(jnp.mean(hidden_rows * hidden_rows, axis=-1, keepdims=True) + eps)
    return hidden_rows * inverse * gain_vector


def gelu_tanh(inputs):
    return (
        0.5 * inputs * (1.0 + jnp.tanh(gelu_scale * (inputs + 0.044715 * inputs * inputs * inputs)))
    )


def gated_unit(gate_pre, up_pre):
    return gelu_tanh(gate_pre) * up_pre


def project(left_side, right_side):
    return jnp.dot(left_side, right_side, preferred_element_type=jnp.float32)


def outer_rows(left_side, right_side):
    return lax.dot_general(
        left_side, right_side, (((0,), (0,)), ((), ())), preferred_element_type=jnp.float32
    )


def back_project(grad_rows, weights):
    return lax.dot_general(
        grad_rows, weights, (((1,), (1,)), ((), ())), preferred_element_type=jnp.float32
    )


def norm_back(hidden_rows, gain_vector, grad_normed):
    unused, pullback = jax.vjp(rms_scale, hidden_rows, gain_vector)
    return pullback(grad_normed)


def attend_forward(queries, keys_in, values_in, allowed):
    scores = jnp.einsum("bqhd,bkhd->bhqk", queries, keys_in, preferred_element_type=jnp.float32)
    scores = jnp.where(allowed, scores, neg_big)
    row_peak = jnp.max(scores, axis=-1, keepdims=True)
    exp_scores = jnp.exp(scores - row_peak)
    row_total = jnp.sum(exp_scores, axis=-1, keepdims=True)
    prob_low = (exp_scores / row_total).astype(jnp.bfloat16)
    mixed_heads = jnp.einsum(
        "bhqk,bkhd->bqhd", prob_low, values_in, preferred_element_type=jnp.float32
    )
    return (mixed_heads.astype(jnp.bfloat16), row_peak + jnp.log(row_total))


def attend_backward(queries, keys_in, values_in, allowed, log_total, grad_mixed):
    scores = jnp.einsum("bqhd,bkhd->bhqk", queries, keys_in, preferred_element_type=jnp.float32)
    scores = jnp.where(allowed, scores, neg_big)
    probs_full = jnp.exp(scores - log_total)
    grad_probs = jnp.einsum(
        "bqhd,bkhd->bhqk", grad_mixed, values_in, preferred_element_type=jnp.float32
    )
    centre = jnp.sum(probs_full * grad_probs, axis=-1, keepdims=True)
    grad_scores = (probs_full * (grad_probs - centre)).astype(jnp.bfloat16)
    grad_queries = jnp.einsum(
        "bhqk,bkhd->bqhd", grad_scores, keys_in, preferred_element_type=jnp.float32
    )
    grad_keys = jnp.einsum(
        "bhqk,bqhd->bkhd", grad_scores, queries, preferred_element_type=jnp.float32
    )
    grad_values = jnp.einsum(
        "bhqk,bqhd->bkhd",
        probs_full.astype(jnp.bfloat16),
        grad_mixed,
        preferred_element_type=jnp.float32,
    )
    return (grad_queries, grad_keys, grad_values)


def split_heads(flat_rows):
    return flat_rows.reshape(1, -1, H, HD)


def swap(piece, axis_name, bit):
    size = lax.axis_size(axis_name)
    return lax.ppermute(piece, axis_name, [(place, place ^ (1 << bit)) for place in range(size)])


def bit_of(axis_name, bit):
    return (lax.axis_index(axis_name) >> bit) & 1


def pick(piece, which, dim):
    return lax.dynamic_index_in_dim(piece, which, dim, keepdims=False)


def halve(piece, axis_name, bit, dim, dtype=jnp.bfloat16):
    mine = bit_of(axis_name, bit)
    received = swap(pick(piece, 1 - mine, dim), axis_name, bit)
    kept = pick(piece, mine, dim)
    return (kept.astype(jnp.float32) + received.astype(jnp.float32)).astype(dtype)


def weight_grads(rows_in, grads, order):
    rows = rows_in.shape[0]
    core = bit_of("narrow", 0)
    parts = [piece.reshape(rows, 2, 2, piece.shape[1] // 4) for piece in grads]
    widths = [piece.shape[3] for piece in parts]

    def side(which):
        picked = [pick(piece, which, 2) for piece in parts]
        return jnp.concatenate(picked, axis=2).reshape(rows, -1)

    away = outer_rows(rows_in, side(1 - core)).astype(jnp.bfloat16)
    received = swap(away, "narrow", 0)
    total = (outer_rows(rows_in, side(core)) + received.astype(jnp.float32)).astype(jnp.bfloat16)
    spread = lax.axis_size("items")
    levels = spread.bit_length() - 1
    height, width = total.shape
    total = total.reshape((2,) * levels + (height // spread, 2, width // 2))
    left = ["x"] + list(range(levels - 1, -1, -1))
    for step, bit in enumerate(order(levels)):
        last = step == levels
        dim = left.index(bit)
        if bit == "x":
            total = halve(total, "narrow", 1, total.ndim - 2, jnp.float32 if last else jnp.bfloat16)
        else:
            total = halve(total, "items", bit, dim - left.index("x") - 1 if "x" in left else dim, jnp.float32 if last else jnp.bfloat16)
        left.remove(bit)
    outs = []
    at = 0
    for width in widths:
        outs.append(total[..., at : at + width].reshape(height // spread, width))
        at += width
    return outs


def order_x(levels):
    return ["x"] + list(range(levels))


def order_y(levels):
    return list(range(levels)) + ["x"]


def order_z(levels):
    return [1, 0] + list(range(2, levels)) + ["x"]


def all_summed(piece):
    for axis_name in ("narrow", "items"):
        for bit in range(lax.axis_size(axis_name).bit_length() - 1):
            piece = piece + swap(piece, axis_name, bit)
    return piece


def to_items(piece):
    return lax.all_to_all(piece, "narrow", split_axis=0, concat_axis=1, tiled=True)


def to_shards(piece):
    return lax.all_to_all(piece, "narrow", split_axis=1, concat_axis=0, tiled=True)


def body(
    tokens,
    memory,
    mem_count,
    cotangent,
    gain_self,
    self_query,
    self_key,
    self_value,
    self_out,
    gain_cross,
    cross_query,
    cross_key,
    cross_value,
    cross_out,
    gain_feed,
    gate_weight,
    up_weight,
    down_weight,
):
    batch_size, local_tok, model_width = tokens.shape
    local_mem = memory.shape[1]
    narrow_count = lax.axis_size("narrow")
    full_tok = local_tok * narrow_count
    full_mem = local_mem * narrow_count
    bf = jnp.bfloat16
    tokens_here = to_items(tokens)
    memory_rows = to_items(memory).reshape(-1, model_width)
    cotangent_rows = to_items(cotangent).reshape(-1, model_width)
    count = pick(mem_count, lax.axis_index("narrow"), 0)
    token_rows = tokens_here.astype(jnp.float32).reshape(-1, model_width)
    normed_one = rms_scale(token_rows, gain_self).astype(bf)
    query_one = project(normed_one, self_query).astype(bf)
    key_one = project(normed_one, self_key).astype(bf)
    value_one = project(normed_one, self_value).astype(bf)
    place = jnp.arange(full_tok, dtype=jnp.int32)
    causal = (place[None, :] <= place[:, None])[None, None]
    attended_one, total_one = attend_forward(
        split_heads(query_one), split_heads(key_one), split_heads(value_one), causal
    )
    attended_flat = attended_one.reshape(-1, model_width)
    hidden_one = token_rows + project(attended_flat, self_out)
    normed_two = rms_scale(hidden_one, gain_cross).astype(bf)
    query_two = project(normed_two, cross_query).astype(bf)
    memory_key = project(memory_rows, cross_key).astype(bf)
    memory_value = project(memory_rows, cross_value).astype(bf)
    patch_live = (jnp.arange(full_mem, dtype=jnp.int32) < count)[None, None, None, :]
    crossed, total_two = attend_forward(
        split_heads(query_two), split_heads(memory_key), split_heads(memory_value), patch_live
    )
    crossed_flat = crossed.reshape(-1, model_width)
    hidden_two = hidden_one + project(crossed_flat, cross_out)
    normed_three = rms_scale(hidden_two, gain_feed).astype(bf)
    gate_pre = project(normed_three, gate_weight)
    up_pre = project(normed_three, up_weight)
    mixed_full, mix_back = jax.vjp(gated_unit, gate_pre, up_pre)
    mixed = mixed_full.astype(bf)
    result = (hidden_two + project(mixed, down_weight)).astype(bf)
    result = to_shards(result[None])
    grad_rows = cotangent_rows.astype(jnp.float32)
    (down_sum,) = weight_grads(mixed, [cotangent_rows], order_z)
    grad_gate, grad_up = mix_back(back_project(cotangent_rows, down_weight))
    grad_gate = grad_gate.astype(bf)
    grad_up = grad_up.astype(bf)
    gate_sum, up_sum = weight_grads(normed_three, [grad_gate, grad_up], order_x)
    grad_normed_three = back_project(grad_gate, gate_weight) + back_project(grad_up, up_weight)
    grad_norm_two, grad_gain_feed = norm_back(hidden_two, gain_feed, grad_normed_three)
    grad_hidden_two = grad_rows + grad_norm_two
    branch_two_grad = grad_hidden_two.astype(bf)
    (cross_out_sum,) = weight_grads(crossed_flat, [branch_two_grad], order_y)
    grad_crossed = back_project(branch_two_grad, cross_out).astype(bf)
    grad_query_two, memory_keys_grad, memory_values_grad = [
        piece.astype(bf).reshape(-1, model_width)
        for piece in attend_backward(
            split_heads(query_two),
            split_heads(memory_key),
            split_heads(memory_value),
            patch_live,
            total_two,
            split_heads(grad_crossed),
        )
    ]
    cross_key_sum, cross_value_sum = weight_grads(
        memory_rows, [memory_keys_grad, memory_values_grad], order_y
    )
    memory_grad = (
        back_project(memory_keys_grad, cross_key) + back_project(memory_values_grad, cross_value)
    ).astype(bf)
    memory_grad = to_shards(memory_grad[None]).astype(jnp.float32)
    (cross_query_sum,) = weight_grads(normed_two, [grad_query_two], order_z)
    grad_norm_one, grad_gain_cross = norm_back(
        hidden_one, gain_cross, back_project(grad_query_two, cross_query)
    )
    grad_hidden_one = grad_hidden_two + grad_norm_one
    branch_one_grad = grad_hidden_one.astype(bf)
    (self_out_sum,) = weight_grads(attended_flat, [branch_one_grad], order_y)
    grad_attended = back_project(branch_one_grad, self_out).astype(bf)
    grad_query_one, key_one_grad, value_one_grad = [
        piece.astype(bf).reshape(-1, model_width)
        for piece in attend_backward(
            split_heads(query_one),
            split_heads(key_one),
            split_heads(value_one),
            causal,
            total_one,
            split_heads(grad_attended),
        )
    ]
    self_query_sum, self_key_sum, self_value_sum = weight_grads(
        normed_one, [grad_query_one, key_one_grad, value_one_grad], order_z
    )
    grad_normed_one = (
        back_project(grad_query_one, self_query)
        + back_project(key_one_grad, self_key)
        + back_project(value_one_grad, self_value)
    )
    grad_norm_zero, grad_gain_self = norm_back(token_rows, gain_self, grad_normed_one)
    tokens_grad = (grad_hidden_one + grad_norm_zero).astype(bf)
    tokens_grad = to_shards(tokens_grad[None]).astype(jnp.float32)
    gains = all_summed(jnp.stack([grad_gain_self, grad_gain_cross, grad_gain_feed]))
    return (
        result,
        tokens_grad,
        memory_grad,
        gains[0],
        self_query_sum,
        self_key_sum,
        self_value_sum,
        self_out_sum,
        gains[1],
        cross_query_sum,
        cross_key_sum,
        cross_value_sum,
        cross_out_sum,
        gains[2],
        gate_sum,
        up_sum,
        down_sum,
    )


def solution(mesh):
    in_specs = (
        P("items", "narrow", None),
        P("items", "narrow", None),
        P("items"),
        P("items", "narrow", None),
        P(),
        P(),
        P(),
        P(),
        P(),
        P(),
        P(),
        P(),
        P(),
        P(),
        P(),
        P(),
        P(),
        P(),
    )
    out_specs = (
        P("items", "narrow", None),
        P("items", "narrow", None),
        P("items", "narrow", None),
        P(),
        P("items", "narrow"),
        P("items", "narrow"),
        P("items", "narrow"),
        P("items", "narrow"),
        P(),
        P("items", "narrow"),
        P("items", "narrow"),
        P("items", "narrow"),
        P("items", "narrow"),
        P(),
        P("items", "narrow"),
        P("items", "narrow"),
        P("items", "narrow"),
    )
    return jax.shard_map(body, mesh=mesh, in_specs=in_specs, out_specs=out_specs, check_vma=False)
```

time: 2040 us -> 801 us (0.39)
  waiting for transfers between devices: 1420 us -> 87.2 us
  other arithmetic: 56.7 us -> 164 us
  starting transfers between devices: 1.67 us -> 71.3 us
  matrix products: 317 us -> 274 us
  blocking collectives: 40.4 us -> 0 us
    reduce_scatter x15 -> x0, waiting for transfers between devices: 1270 us -> none  [the longest x1 121 us: body(): lax.psum_scatter(flat_grids[9], ('items', 'narrow'), scatter_dimension=0,...]
    all_gather x4 -> x0, waiting for transfers between devices: 153 us -> none  [the longest x1 67 us: body(): lax.all_gather(memory_key, 'narrow', axis=1, tiled=True)]
    ppermute x0 -> x40, waiting for transfers between devices: none -> 65.1 us  [swap(): lax.ppermute(piece, axis_name, [(place, place ^ 1 << bit) for place in ra...]
    unnamed x0 -> x4, other arithmetic: none -> 47.9 us
    ppermute x0 -> x40, starting transfers between devices: none -> 44 us  [swap(): lax.ppermute(piece, axis_name, [(place, place ^ 1 << bit) for place in ra...]
    all_gather x4 -> x0, local copies, waits for them, and re-layouts: 42.7 us -> none  [the longest x1 16.8 us: body(): lax.all_gather(memory_key, 'narrow', axis=1, tiled=True)]
    dynamic_slice x8 -> x15, local copies, waits for them, and re-layouts: 0.32 us -> 41.2 us  [pick(): return lax.dynamic_index_in_dim(piece, which, dim, keepdims=False)]
    psum x1 -> x0, blocking collectives: 40.4 us -> none  [body(): lax.psum((grad_gain_self, grad_gain_cross, grad_gain_feed), ('items', 'na...]
  transfers between devices with their start and end apart: 19 -> 46, of which waited for: 17 -> 18; matrix products, arithmetic and copies ran while one was open for 13% -> 40% of each run, Pallas kernels for 0% -> 0%
where the time goes in v1:
time: 801 us; the launch traced here: 792 us
  matrix products  274 us (34%)
  local copies, waits for them, and re-layouts  193 us (24%)
  other arithmetic  164 us (20%)
  waiting for transfers between devices  87.2 us (11%)
  starting transfers between devices  71.3 us (9%)
    ppermute x40, waiting for transfers between devices, swap(): lax.ppermute(piece, axis_name, [(place, place ^ 1 << bit) for place in ra...  65.1 us
    unnamed x208, local copies, waits for them, and re-layouts  52.6 us
    unnamed x4, other arithmetic  47.9 us
    convert_element_type x2, other arithmetic, attend_backward(): grad_scores = (probs_full * (grad_probs - centre)).astype(jnp.bfloat16)  47.7 us
    dot_general x14, matrix products, outer_rows(): lax.dot_general(left_side, right_side, (((0,), (0,)), ((), ())), preferre...  47.3 us
    ppermute x40, starting transfers between devices, swap(): lax.ppermute(piece, axis_name, [(place, place ^ 1 << bit) for place in ra...  44 us
    dot_general x2, matrix products, attend_backward(): jnp.einsum('bqhd,bkhd->bhqk', grad_mixed, values_in, preferred_element_ty...  43.9 us
    dynamic_slice x15, local copies, waits for them, and re-layouts, pick(): return lax.dynamic_index_in_dim(piece, which, dim, keepdims=False)  41.2 us
  transfers between devices with their start and end apart: 46, of which 18 were waited for; matrix products, arithmetic and copies ran while one was open for 40% of the time, Pallas kernels for 0%

profile of v1, /device:TPU:0, one launch (start us, length us, event | category | flops | bytes accessed | tf_op | source)
XLA Modules:
  0.0 791.7 jit_solution(14579592683567269993)
XLA Ops:
  0.7 4.5 all-to-all-start
  7.2 10.3 %all-to-all-done = bf16[4,128,768]{2,1,0:T(8,128)(2,1)} async-done(((bf16[4,128,768]{2,1,0:T(8,128)(2,1)}), bf16[4,128,768]{2,1,0:T(8,128)(2,1)}, u32[]{:S(2)}, u32[]{:S(2)}) %all-to-all-start) | async-done | bytes 786464 | tf_op jit(solution)/shard_map/all_to_all | solution.py:166
  17.5 4.2 all-to-all-start.3
  42.4 4.5 copy-done.1
  49.1 4.9 all-to-all-start.1
  54.0 8.9 %fusion.47 = bf16[12,64,512]{2,1,0:T(8,128)(2,1)} fusion(bf16[512,12,64]{0,2,1:T(8,128)(2,1)} %bitcast.459, f32[12,512,512]{1,2,0:T(8,128)} %copy-done.1, f32[12,512]{1,0:T(8,128)S(1)} %fusion.8, f32[12,512]{1,0:T(8,128)S(1)} %get-tuple-element.76, pred[512,512]{0,1:T(8,128)(4,1)S(1)} %iota_compare_fusion), kind=kOutput, calls=%fused_computation.116 | convolution fusion | flops 415629312 | bytes 14467072 | tf_op jit(solution)/shard_map/bhqk,bkhd->bqhd/dot_general | solution.py:58
  79.2 11.7 %all-to-all-done.1 = bf16[4,512,768]{2,1,0:T(8,128)(2,1)} async-done(((bf16[4,512,768]{2,1,0:T(8,128)(2,1)}), bf16[4,512,768]{2,1,0:T(8,128)(2,1)}, u32[]{:S(2)}, u32[]{:S(2)}) %all-to-all-start.1) | async-done | bytes 3145760 | tf_op jit(solution)/shard_map/all_to_all | solution.py:166
  91.0 6.6 convolution_convert_fusion.2
  97.6 5.9 convolution_convert_fusion.3
  103.6 21.9 %select_reduce_fusion = (f32[12,512]{1,0:T(8,128)S(1)}, f32[12,512,2048]{2,1,0:T(8,128)}) fusion(pred[2048]{0:T(1024)(128)(4,1)S(1)} %iota_compare_fusion.1, bf16[512,12,64]{0,2,1:T(8,128)(2,1)} %bitcast.435, bf16[2048,12,64]{0,2,1:T(8,128)(2,1)} %bitcast.427), kind=kOutput, calls=%fused_computation.6 | convolution fusion | flops 1635772416 | bytes 54290432 | tf_op jit(solution)/shard_map/bqhd,bkhd->bhqk/dot_general | solution.py:52
  125.4 20.7 %fusion = f32[12,512]{1,0:T(8,128)S(1)} fusion(f32[12,512,2048]{2,1,0:T(8,128)} %get-tuple-element.81, f32[12,512]{1,0:T(8,128)S(1)} %get-tuple-element.80, pred[2048]{0:T(1024)(128)(4,1)S(1)} %iota_compare_fusion.1), kind=kLoop, calls=%fused_computation.5 | loop fusion | flops 37742592 | bytes 50382848 | tf_op jit(solution)/shard_map/reduce_sum | solution.py:56
  146.7 19.9 %fusion.48 = bf16[12,64,512]{2,1,0:T(8,128)(2,1)S(1)} fusion(bf16[2048,12,64]{0,2,1:T(8,128)(2,1)S(1)} %bitcast.458, f32[12,512,2048]{2,1,0:T(8,128)} %get-tuple-element.81, f32[12,512]{1,0:T(8,128)} %copy-done.65, f32[12,512]{1,0:T(8,128)S(1)} %get-tuple-element.80, pred[2048]{0:T(1024)(128)(4,1)S(1)} %iota_compare_fusion.1), kind=kOutput, calls=%fused_computation.117 | convolution fusion | flops 1661337600 | bytes 54315008 | tf_op jit(solution)/shard_map/bhqk,bkhd->bqhd/dot_general | solution.py:58
  173.5 8.3 %multiply_convert_fusion.2 = (bf16[512,2048]{1,0:T(8,128)(2,1)}, bf16[512,2048]{1,0:T(8,128)(2,1)S(1)}, bf16[512,2048]{1,0:T(8,128)(2,1)}) fusion(f32[512,2048]{1,0:T(8,128)S(1)} %fusion.81, f32[512,2048]{1,0:T(8,128)S(1)} %fusion.82, bf16[512,768]{1,0:T(8,128)(2,1)} %bitcast.17, bf16[2048,768]{1,0:T(8,128)(2,1)S(1)} %copy-done), kind=kOutput, calls=%fused_computation.38 | convolution fusion | flops 1642070016 | bytes 18612224 | tf_op jit(solution)/shard_map/dot_general | solution.py:41
  186.2 4.5 reshape.581
  190.7 4.5 reshape.582
  195.1 5.6 multiply_reduce_fusion.2
  212.2 20.6 %fusion.22 = bf16[12,64,2048]{2,1,0:T(8,128)(2,1)} fusion(bf16[512,12,64]{0,2,1:T(8,128)(2,1)} %bitcast.437, f32[12,512,2048]{2,1,0:T(8,128)} %get-tuple-element.81, f32[12,512]{1,0:T(8,128)S(1)} %log_add_fusion.1, pred[2048]{0:T(1024)(128)(4,1)S(1)} %iota_compare_fusion.1), kind=kOutput, calls=%fused_computation.46 | convolution fusion | flops 1649934336 | bytes 54290432 | tf_op jit(solution)/shard_map/bhqk,bqhd->bkhd/dot_general | solution.py:79
  232.8 34.6 %multiply_reduce_fusion = (f32[12,512]{1,0:T(8,128)S(1)}, f32[12,512,2048]{2,1,0:T(8,128)}) fusion(f32[12,512,2048]{2,1,0:T(8,128)} %get-tuple-element.81, f32[12,512]{1,0:T(8,128)S(1)} %log_add_fusion.1, pred[2048]{0:T(1024)(128)(4,1)S(1)} %iota_compare_fusion.1, bf16[512,12,64]{0,2,1:T(8,128)(2,1)} %bitcast.438, bf16[2048,12,64]{0,2,1:T(8,128)(2,1)} %bitcast.457), kind=kOutput, calls=%fused_computation.1 | convolution fusion | flops 1660938240 | bytes 104646656 | tf_op jit(solution)/shard_map/bqhd,bkhd->bhqk/dot_general | solution.py:68
  267.4 40.5 %multiply_convert_fusion = bf16[12,512,2048]{2,1,0:T(8,128)(2,1)} fusion(f32[12,512,2048]{2,1,0:T(8,128)} %get-tuple-element.86, f32[12,512,2048]{2,1,0:T(8,128)} %get-tuple-element.81, f32[12,512]{1,0:T(8,128)S(1)} %get-tuple-element.85, f32[12,512]{1,0:T(8,128)S(1)} %log_add_fusion.1, pred[2048]{0:T(1024)(128)(4,1)S(1)} %iota_compare_fusion.1), kind=kLoop, calls=%fused_computation | loop fusion | flops 62914560 | bytes 125880320 | tf_op jit(solution)/shard_map/convert_element_type | solution.py:72
  307.9 14.6 %convolution_convert_fusion.7 = bf16[12,64,512]{2,1,0:T(8,128)(2,1)} fusion(bf16[2048,12,64]{0,2,1:T(8,128)(2,1)} %bitcast.428, bf16[12,512,2048]{2,1,0:T(8,128)(2,1)} %multiply_convert_fusion), kind=kOutput, calls=%fused_computation.105 | convolution fusion | flops 1611005952 | bytes 29097984 | tf_op jit(solution)/shard_map/bhqk,bkhd->bqhd/dot_general | solution.py:73
  322.5 14.7 %convolution_convert_fusion.4 = bf16[12,64,2048]{2,1,0:T(8,128)(2,1)} fusion(bf16[512,12,64]{0,2,1:T(8,128)(2,1)} %bitcast.436, bf16[12,512,2048]{2,1,0:T(8,128)(2,1)} %multiply_convert_fusion), kind=kOutput, calls=%fused_computation.47 | convolution fusion | flops 1612185600 | bytes 29097984 | tf_op jit(solution)/shard_map/bhqk,bqhd->bkhd/dot_general | solution.py:76
  339.1 3.3 fusion.76
  350.4 8.6 %fusion.44 = bf16[12,64,512]{2,1,0:T(8,128)(2,1)} fusion(bf16[512,12,64]{0,2,1:T(8,128)(2,1)} %bitcast.461, f32[12,512,512]{1,2,0:T(8,128)} %copy-done.1, f32[12,512]{1,0:T(8,128)S(1)} %copy-done.64, pred[512,512]{0,1:T(8,128)(4,1)S(1)} %copy-done.24), kind=kOutput, calls=%fused_computation.113 | convolution fusion | flops 412483584 | bytes 14442496 | tf_op jit(solution)/shard_map/bhqk,bqhd->bkhd/dot_general | solution.py:79
  359.0 9.3 %multiply_reduce_fusion.1 = (f32[12,512]{1,0:T(8,128)S(1)}, f32[12,512,512]{1,2,0:T(8,128)}) fusion(f32[12,512,512]{1,2,0:T(8,128)} %copy-done.1, f32[12,512]{1,0:T(8,128)S(1)} %copy-done.64, pred[512,512]{0,1:T(8,128)(4,1)S(1)} %copy-done.24, bf16[512,12,64]{0,2,1:T(8,128)(2,1)S(1)} %bitcast.462, bf16[512,12,64]{0,2,1:T(8,128)(2,1)S(1)} %bitcast.460), kind=kOutput, calls=%fused_computation.14 | convolution fusion | flops 415229952 | bytes 27049984 | tf_op jit(solution)/shard_map/bqhd,bkhd->bhqk/dot_general | solution.py:68
  368.3 7.2 multiply_convert_fusion.1
  385.2 7.3 reduce.22
  394.5 4.2 all-to-all-start.2
  405.7 9.7 %constant_dynamic-slice_fusion.6 = (bf16[512,2,1,512]{3,2,1,0:T(2,128)(2,1)S(1)}, bf16[512,2,1,512]{3,2,1,0:T(2,128)(2,1)}, bf16[512,2,1,512]{3,2,1,0:T(2,128)(2,1)}, bf16[512,2,1,512]{3,2,1,0:T(2,128)(2,1)S(1)}) fusion(bf16[512,2,2,512]{3,2,1,0:T(2,128)(2,1)S(1)} %copy-done.7, s32[]{:T(128)S(6)} %select_n.142, s32[]{:T(128)S(6)} %select_n.141, ...), kind=kLoop, calls=%fused_computation.221 | loop fusion | bytes 8388616 | tf_op jit(solution)/shard_map/jit(dynamic_index_in_dim)/dynamic_slice | solution.py:102
  417.7 4.3 copy.192
  422.0 5.5 convolution_convert_fusion
  434.8 5.7 fusion.43
  446.0 4.4 fusion.26
  472.6 4.0 copy.189
  476.6 6.8 copy.265
  483.4 33.4 %reduce.24 = bf16[2048,768]{1,0:T(8,128)(2,1)} reduce(bf16[2048,1,768]{2,1,0:T(2,128)(2,1)} %bitcast.425, bf16[]{:T(256)} %broadcast.221), dimensions={1}, to_apply=%bitcast.420.reduce_sub_computation | reduce | bytes 6291458
  516.8 4.7 reshape.627
  521.4 3.5 copy.266
  524.9 7.3 reduce.23
  538.9 4.6 all-to-all-start.4
  543.5 3.7 reshape.624
  575.4 4.9 all-to-all-start.5
  580.3 3.7 reshape.626
  590.8 7.5 collective-permute-done.16
  600.1 4.9 collective-permute-done.27
  606.6 4.2 collective-permute-done.12
  612.3 4.1 collective-permute-done.17
  616.9 7.4 collective-permute-done.28
  624.3 7.3 collective-permute-done.13
  631.7 5.8 collective-permute-done.18
  640.1 5.7 fusion.27
  648.2 3.6 reshape.576
  665.1 3.9 add_convert_fusion.3
  671.7 3.8 reshape.588
  682.8 3.9 add_convert_fusion.2
  686.8 5.4 reshape.566
  695.5 3.9 constant_dynamic-slice_fusion.24
  703.7 5.4 add_convert_fusion
  709.1 6.3 reshape.585
  715.5 11.1 %constant_dynamic-slice_fusion.5 = (bf16[2,2,2,96,1,1024]{5,4,3,2,1,0:T(2,128)(2,1)}, bf16[2,2,2,96,1,1024]{5,4,3,2,1,0:T(2,128)(2,1)S(1)}) fusion(bf16[2,2,2,96,2,1024]{5,4,3,2,1,0:T(2,128)(2,1)} %reshape.585, s32[]{:T(128)S(6)} %select_n.149, s32[]{:T(128)S(6)} %select_n.150), kind=kLoop, calls=%fused_computation.220 | loop fusion | bytes 6291464 | tf_op jit(solution)/shard_map/jit(dynamic_index_in_dim)/dynamic_slice | solution.py:102
  740.7 6.4 reshape.628
  747.1 6.0 copy.205
  765.5 5.7 collective-permute-done.8
  776.3 5.3 collective-permute-done.33
  784.3 6.2 collective-permute-done.34
  (426 shorter events, 247.7 us)
Async XLA Ops:
  0.7 172.8 %copy-start = (bf16[2048,768]{1,0:T(8,128)(2,1)S(1)}, bf16[2048,768]{1,0:T(8,128)(2,1)}, u32[]{:S(2)}) copy-start(bf16[2048,768]{1,0:T(8,128)(2,1)} %param.35) | copy-start | bytes 9437188
  0.7 22.5 %copy-start.66 = (f32[768]{0:T(1024)S(1)}, f32[768]{0:T(1024)}, u32[]{:S(2)}) copy-start(f32[768]{0:T(1024)} %param.22) | copy-start | bytes 9220
  0.7 16.8 %all-to-all-start = ((bf16[4,128,768]{2,1,0:T(8,128)(2,1)}), bf16[4,128,768]{2,1,0:T(8,128)(2,1)}, u32[]{:S(2)}, u32[]{:S(2)}) async-start(bf16[4,128,768]{2,1,0:T(8,128)(2,1)} %param.18), calls=%async_computation | async-start | bytes 1572864 | tf_op jit(solution)/shard_map/all_to_all | solution.py:166
  7.2 46.8 %copy-start.23 = (pred[512,512]{0,1:T(8,128)(4,1)}, pred[512,512]{0,1:T(8,128)(4,1)S(1)}, u32[]{:S(2)}) copy-start(pred[512,512]{0,1:T(8,128)(4,1)S(1)} %iota_compare_fusion) | copy-start | bytes 786436
  17.5 31.6 %all-to-all-start.3 = ((bf16[4,128,768]{2,1,0:T(8,128)(2,1)}), bf16[4,128,768]{2,1,0:T(8,128)(2,1)}, u32[]{:S(2)}, u32[]{:S(2)}) async-start(bf16[4,128,768]{2,1,0:T(8,128)(2,1)} %param.21), calls=%async_computation.3 | async-start | bytes 1572864 | tf_op jit(solution)/shard_map/all_to_all | solution.py:166
  23.2 53.1 %copy-start.70 = (f32[4,128]{1,0:T(4,128)}, f32[4,128]{1,0:T(4,128)S(1)}, u32[]{:S(2)}) copy-start(f32[4,128]{1,0:T(4,128)S(1)} %fusion.39) | copy-start | bytes 6148
  49.1 41.9 %all-to-all-start.1 = ((bf16[4,512,768]{2,1,0:T(8,128)(2,1)}), bf16[4,512,768]{2,1,0:T(8,128)(2,1)}, u32[]{:S(2)}, u32[]{:S(2)}) async-start(bf16[4,512,768]{2,1,0:T(8,128)(2,1)} %param.19), calls=%async_computation.1 | async-start | bytes 6291456 | tf_op jit(solution)/shard_map/all_to_all | solution.py:166
  125.4 21.3 %copy-start.36 = (bf16[2048,768]{0,1:T(8,128)(2,1)S(1)}, bf16[2048,768]{0,1:T(8,128)(2,1)}, u32[]{:S(2)}) copy-start(bf16[2048,768]{0,1:T(8,128)(2,1)} %convolution_convert_fusion.3) | copy-start | bytes 9437188
  146.7 20.0 %copy-start.10 = (f32[512,768]{1,0:T(8,128)S(1)}, f32[512,768]{1,0:T(8,128)}, u32[]{:S(2)}) copy-start(f32[512,768]{1,0:T(8,128)} %copy-done.9) | copy-start | bytes 4718596
  146.7 20.0 %copy-start.53 = (bf16[768,768]{1,0:T(8,128)(2,1)S(1)}, bf16[768,768]{1,0:T(8,128)(2,1)}, u32[]{:S(2)}) copy-start(bf16[768,768]{1,0:T(8,128)(2,1)} %param.31) | copy-start | bytes 3538948
  322.5 14.7 %copy-start.11 = (f32[512,768]{1,0:T(8,128)S(1)}, f32[512,768]{1,0:T(8,128)}, u32[]{:S(2)}) copy-start(f32[512,768]{1,0:T(8,128)} %copy-done.9) | copy-start | bytes 4718596
  322.5 14.7 %copy-start.31 = (bf16[12,64,512]{2,1,0:T(8,128)(2,1)S(1)}, bf16[12,64,512]{2,1,0:T(8,128)(2,1)}, u32[]{:S(2)}) copy-start(bf16[12,64,512]{2,1,0:T(8,128)(2,1)} %convolution_convert_fusion.7) | copy-start | bytes 2359300
  322.5 14.7 %copy-start.75 = (f32[512]{0:T(512)S(1)}, f32[512]{0:T(512)}, u32[]{:S(2)}) copy-start(f32[512]{0:T(512)} %copy-done.74) | copy-start | bytes 6148
  322.5 14.7 %copy-start.77 = (f32[768]{0:T(1024)S(1)}, f32[768]{0:T(1024)}, u32[]{:S(2)}) copy-start(f32[768]{0:T(1024)} %param.27) | copy-start | bytes 9220
  322.5 14.7 %copy-start.83 = (bf16[768,768]{1,0:T(8,128)(2,1)S(1)}, bf16[768,768]{1,0:T(8,128)(2,1)}, u32[]{:S(2)}) copy-start(bf16[768,768]{1,0:T(8,128)(2,1)} %param.28) | copy-start | bytes 3538948
  350.4 17.9 %slice-start = ((s8[12582912]{0:T(1024)(128)(4,1)}), s8[4194304]{0:T(1024)(128)(4,1)S(1)}, s32[]{:S(2)}) async-start(s8[12582912]{0:T(1024)(128)(4,1)} %bitcast.423), calls=%async_computation.6 | async-start | bytes 8388608
  350.4 17.9 %slice-start.1 = ((s8[12582912]{0:T(1024)(128)(4,1)}), s8[4194304]{0:T(1024)(128)(4,1)S(1)}, s32[]{:S(2)}) async-start(s8[12582912]{0:T(1024)(128)(4,1)} %bitcast.423), calls=%async_computation.7 | async-start | bytes 8388608
  394.5 144.4 %all-to-all-start.2 = ((bf16[4,2,49152]{2,1,0:T(2,128)(2,1)}), bf16[4,2,49152]{2,1,0:T(2,128)(2,1)}, u32[]{:S(2)}, u32[]{:S(2)}) async-start(bf16[4,2,49152]{2,1,0:T(2,128)(2,1)} %reshape.623), calls=%async_computation.2 | async-start | bytes 1572864 | tf_op jit(solution)/shard_map/all_to_all | solution.py:170
  402.7 132.8 %collective-permute-start.25 = (bf16[768,384]{1,0:T(8,128)(2,1)}, bf16[768,384]{1,0:T(8,128)(2,1)}, u32[]{:S(2)}, u32[]{:S(2)}) collective-permute-start(bf16[768,384]{1,0:T(8,128)(2,1)} %convolution_convert_fusion.16), channel_id=1, source_target_pairs={{0,1},{1,0},{2,3},{3,2},{4,5},{5,4},{6,7},{7,6},{8,9},{9,8},{10,11... | collective-permute-start | bytes 1769480 | tf_op jit(solution)/shard_map/ppermute | solution.py:94
  405.6 259.5 %collective-permute-start.35 = (bf16[2048,384]{1,0:T(8,128)(2,1)}, bf16[2048,384]{1,0:T(8,128)(2,1)}, u32[]{:S(2)}, u32[]{:S(2)}) collective-permute-start(bf16[2048,384]{1,0:T(8,128)(2,1)} %convolution_convert_fusion.5), channel_id=1, source_target_pairs={{0,1},{1,0},{2,3},{3,2},{4,5},{5,4},{6,7},{7,6},{8,9},{9,8},{10,11... | collective-permute-start | bytes 4718600 | tf_op jit(solution)/shard_map/ppermute | solution.py:94
  427.5 276.2 %collective-permute-start.30 = (bf16[768,2048]{1,0:T(8,128)(2,1)}, bf16[768,2048]{1,0:T(8,128)(2,1)}, u32[]{:S(2)}, u32[]{:S(2)}) collective-permute-start(bf16[768,2048]{1,0:T(8,128)(2,1)} %convolution_convert_fusion), channel_id=1, source_target_pairs={{0,1},{1,0},{2,3},{3,2},{4,5},{5,4},{6,7},{7,6},{8,9},{9,8},{10,11... | collective-permute-start | bytes 9437192 | tf_op jit(solution)/shard_map/ppermute | solution.py:94
  430.2 126.0 %collective-permute-start.10 = (bf16[768,384]{1,0:T(8,128)(2,1)}, bf16[768,384]{1,0:T(8,128)(2,1)}, u32[]{:S(2)}, u32[]{:S(2)}) collective-permute-start(bf16[768,384]{1,0:T(8,128)(2,1)} %convolution_convert_fusion.18), channel_id=1, source_target_pairs={{0,1},{1,0},{2,3},{3,2},{4,5},{5,4},{6,7},{7,6},{8,9},{9,8},{10,11... | collective-permute-start | bytes 1769480 | tf_op jit(solution)/shard_map/ppermute | solution.py:94
  445.7 11.1 %collective-permute-start = (f32[3,768]{1,0:T(4,128)S(1)}, f32[3,768]{1,0:T(4,128)S(1)}, u32[]{:S(2)}, u32[]{:S(2)}) collective-permute-start(f32[3,768]{1,0:T(4,128)S(1)} %pad_maximum_fusion.6), channel_id=1, source_target_pairs={{0,1},{1,0},{2,3},{3,2},{4,5},{5,4},{6,7},{7,6},{8,9},{9,8},{10,11... | collective-permute-start | bytes 27656 | tf_op jit(solution)/shard_map/ppermute | solution.py:94
  456.8 3.8 collective-permute-start.1
  460.6 4.5 collective-permute-start.2
  465.2 3.8 collective-permute-start.3
  468.9 65.3 %collective-permute-start.4 = (f32[3,768]{1,0:T(4,128)S(1)}, f32[3,768]{1,0:T(4,128)}, u32[]{:S(2)}, u32[]{:S(2)}) collective-permute-start(f32[3,768]{1,0:T(4,128)S(1)} %add.363), channel_id=1, source_target_pairs={{0,16},{4,20},{8,24},{12,28},{16,0},{20,4},{24,8},{28,12},{1,17},{... | collective-permute-start | bytes 27656 | tf_op jit(solution)/shard_map/ppermute | solution.py:94
  534.2 32.5 %collective-permute-start.15 = (bf16[768,384]{1,0:T(8,128)(2,1)}, bf16[768,384]{1,0:T(8,128)(2,1)}, u32[]{:S(2)}, u32[]{:S(2)}) collective-permute-start(bf16[768,384]{1,0:T(8,128)(2,1)} %convolution_convert_fusion.17), channel_id=1, source_target_pairs={{0,1},{1,0},{2,3},{3,2},{4,5},{5,4},{6,7},{7,6},{8,9},{9,8},{10,11... | collective-permute-start | bytes 1769480 | tf_op jit(solution)/shard_map/ppermute | solution.py:94
  535.5 103.7 %collective-permute-start.20 = (bf16[768,768]{0,1:T(8,128)(2,1)}, bf16[768,768]{0,1:T(8,128)(2,1)}, u32[]{:S(2)}, u32[]{:S(2)}) collective-permute-start(bf16[768,768]{0,1:T(8,128)(2,1)} %fusion.43), channel_id=1, source_target_pairs={{0,1},{1,0},{2,3},{3,2},{4,5},{5,4},{6,7},{7,6},{8,9},{9,8},{10,11... | collective-permute-start | bytes 3538952 | tf_op jit(solution)/shard_map/ppermute | solution.py:94
  538.9 36.5 %all-to-all-start.4 = ((bf16[4,2,49152]{2,1,0:T(2,128)(2,1)}), bf16[4,2,49152]{2,1,0:T(2,128)(2,1)}, u32[]{:S(2)}, u32[]{:S(2)}) async-start(bf16[4,2,49152]{2,1,0:T(2,128)(2,1)} %reshape.625), calls=%async_computation.4 | async-start | bytes 1572864 | tf_op jit(solution)/shard_map/all_to_all | solution.py:170
  556.2 30.6 %collective-permute-start.26 = (bf16[2,2,96,2,192]{4,2,3,0,1:T(8,128)(2,1)}, bf16[2,2,96,2,192]{4,2,3,0,1:T(8,128)(2,1)}, u32[]{:S(2)}, u32[]{:S(2)}) collective-permute-start(bf16[2,2,96,2,192]{4,2,3,0,1:T(8,128)(2,1)} %bitcast.415), channel_id=1, source_target_pairs={{0,4},{4,0},{8,12},{12,8},{16,20},{20,16},{24,28},{28,24},{1,5},{5... | collective-permute-start | bytes 884744 | tf_op jit(solution)/shard_map/ppermute | solution.py:94
  566.7 22.8 %collective-permute-start.11 = (bf16[2,2,96,2,192]{4,2,3,0,1:T(8,128)(2,1)}, bf16[2,2,96,2,192]{4,2,3,0,1:T(8,128)(2,1)}, u32[]{:S(2)}, u32[]{:S(2)}) collective-permute-start(bf16[2,2,96,2,192]{4,2,3,0,1:T(8,128)(2,1)} %bitcast.417), channel_id=1, source_target_pairs={{0,4},{4,0},{8,12},{12,8},{16,20},{20,16},{24,28},{28,24},{1,5},{5... | collective-permute-start | bytes 884744 | tf_op jit(solution)/shard_map/ppermute | solution.py:94
  575.4 165.2 %all-to-all-start.5 = ((bf16[4,2,196608]{2,1,0:T(2,128)(2,1)}), bf16[4,2,196608]{2,1,0:T(2,128)(2,1)}, u32[]{:S(2)}, u32[]{:S(2)}) async-start(bf16[4,2,196608]{2,1,0:T(2,128)(2,1)} %reshape.627), calls=%async_computation.5 | async-start | bytes 6291456 | tf_op jit(solution)/shard_map/all_to_all | solution.py:170
  586.8 11.5 %collective-permute-start.16 = (bf16[2,2,96,2,192]{4,2,3,0,1:T(8,128)(2,1)S(1)}, bf16[2,2,96,2,192]{4,2,3,0,1:T(8,128)(2,1)S(1)}, u32[]{:S(2)}, u32[]{:S(2)}) collective-permute-start(bf16[2,2,96,2,192]{4,2,3,0,1:T(8,128)(2,1)S(1)} %bitcast.490), channel_id=1, source_target_pairs={{0,8},{4,12},{8,0},{12,4},{16,24},{20,28},{24,16},{28,20},{1,9},{5... | collective-permute-start | bytes 884744 | tf_op jit(solution)/shard_map/ppermute | solution.py:94
  589.5 93.3 %collective-permute-start.5 = (bf16[768,1152]{1,0:T(8,128)(2,1)}, bf16[768,1152]{1,0:T(8,128)(2,1)}, u32[]{:S(2)}, u32[]{:S(2)}) collective-permute-start(bf16[768,1152]{1,0:T(8,128)(2,1)} %convolution_convert_fusion.1), channel_id=1, source_target_pairs={{0,1},{1,0},{2,3},{3,2},{4,5},{5,4},{6,7},{7,6},{8,9},{9,8},{10,11... | collective-permute-start | bytes 5308424 | tf_op jit(solution)/shard_map/ppermute | solution.py:94
  598.3 6.6 collective-permute-start.27
  600.0 40.2 %copy-start.39 = (bf16[2048,2,384]{0,2,1:T(8,128)(2,1)S(1)}, bf16[2048,2,384]{0,2,1:T(8,128)(2,1)}, u32[]{:S(2)}) copy-start(bf16[2048,2,384]{0,2,1:T(8,128)(2,1)} %pad_maximum_fusion) | copy-start | bytes 9437188
  604.9 5.8 collective-permute-start.12
  610.7 5.7 collective-permute-start.17
  616.4 7.8 collective-permute-start.28
  624.2 7.4 collective-permute-start.13
  631.6 5.8 collective-permute-start.18
  637.4 16.0 %collective-permute-start.29 = (bf16[96,192]{1,0:T(8,128)(2,1)S(1)}, bf16[96,192]{1,0:T(8,128)(2,1)}, u32[]{:S(2)}, u32[]{:S(2)}) collective-permute-start(bf16[96,192]{1,0:T(8,128)(2,1)S(1)} %dynamic-slice_bitcast_fusion.27), channel_id=1, source_target_pairs={{0,2},{1,3},{2,0},{3,1},{4,6},{5,7},{6,4},{7,5},{8,10},{9,11},{10,... | collective-permute-start | bytes 110600 | tf_op jit(solution)/shard_map/ppermute | solution.py:94
  639.3 17.2 %collective-permute-start.14 = (bf16[96,192]{1,0:T(8,128)(2,1)S(1)}, bf16[96,192]{1,0:T(8,128)(2,1)}, u32[]{:S(2)}, u32[]{:S(2)}) collective-permute-start(bf16[96,192]{1,0:T(8,128)(2,1)S(1)} %dynamic-slice_bitcast_fusion.29), channel_id=1, source_target_pairs={{0,2},{1,3},{2,0},{3,1},{4,6},{5,7},{6,4},{7,5},{8,10},{9,11},{10,... | collective-permute-start | bytes 110600 | tf_op jit(solution)/shard_map/ppermute | solution.py:94
  651.8 11.6 %copy-start.30 = (bf16[2,2,2,96,2,384]{5,4,3,2,1,0:T(2,128)(2,1)S(1)}, bf16[2,2,2,96,2,384]{5,4,3,2,1,0:T(2,128)(2,1)}, u32[]{:S(2)}) copy-start(bf16[2,2,2,96,2,384]{5,4,3,2,1,0:T(2,128)(2,1)} %reshape.576) | copy-start | bytes 3538948
  651.8 13.3 %copy-start.63 = (bf16[512,2,1,192]{0,3,2,1:T(8,128)(2,1)S(1)}, bf16[512,2,1,192]{0,3,2,1:T(8,128)(2,1)}, u32[]{:S(2)}) copy-start(bf16[512,2,1,192]{0,3,2,1:T(8,128)(2,1)} %get-tuple-element.46) | copy-start | bytes 1179652
  651.8 13.3 %copy-start.92 = (bf16[512,2048]{1,0:T(8,128)(2,1)S(1)}, bf16[512,2048]{1,0:T(8,128)(2,1)}, u32[]{:S(2)}) copy-start(bf16[512,2048]{1,0:T(8,128)(2,1)} %get-tuple-element.30) | copy-start | bytes 6291460
  653.5 9.9 %collective-permute-start.21 = (bf16[2,2,96,2,384]{4,3,2,1,0:T(2,128)(2,1)S(1)}, bf16[2,2,96,2,384]{4,3,2,1,0:T(2,128)(2,1)S(1)}, u32[]{:S(2)}, u32[]{:S(2)}) collective-permute-start(bf16[2,2,96,2,384]{4,3,2,1,0:T(2,128)(2,1)S(1)} %dynamic-slice_bitcast_fusion.6), channel_id=1, source_target_pairs={{0,4},{4,0},{8,12},{12,8},{16,20},{20,16},{24,28},{28,24},{1,5},{5... | collective-permute-start | bytes 1769480 | tf_op jit(solution)/shard_map/ppermute | solution.py:94
  656.5 4.3 collective-permute-start.19
  665.0 15.2 %collective-permute-start.22 = (bf16[2,96,2,384]{3,2,1,0:T(2,128)(2,1)S(1)}, bf16[2,96,2,384]{3,2,1,0:T(2,128)(2,1)}, u32[]{:S(2)}, u32[]{:S(2)}) collective-permute-start(bf16[2,96,2,384]{3,2,1,0:T(2,128)(2,1)S(1)} %dynamic-slice_bitcast_fusion.15), channel_id=1, source_target_pairs={{0,8},{4,12},{8,0},{12,4},{16,24},{20,28},{24,16},{28,20},{1,9},{5... | collective-permute-start | bytes 884744 | tf_op jit(solution)/shard_map/ppermute | solution.py:94
  678.2 50.9 %collective-permute-start.36 = (bf16[2,2,256,2,192]{2,1,0,4,3:T(2,128)(2,1)}, bf16[2,2,256,2,192]{2,1,0,4,3:T(2,128)(2,1)}, u32[]{:S(2)}, u32[]{:S(2)}) collective-permute-start(bf16[2,2,256,2,192]{2,1,0,4,3:T(2,128)(2,1)} %dynamic-slice_bitcast_fusion.4), channel_id=1, source_target_pairs={{0,8},{4,12},{8,0},{12,4},{16,24},{20,28},{24,16},{28,20},{1,9},{5... | collective-permute-start | bytes 2359304 | tf_op jit(solution)/shard_map/ppermute | solution.py:94
  682.4 10.6 %collective-permute-start.23 = (bf16[96,2,384]{2,1,0:T(2,128)(2,1)}, bf16[96,2,384]{2,1,0:T(2,128)(2,1)}, u32[]{:S(2)}, u32[]{:S(2)}) collective-permute-start(bf16[96,2,384]{2,1,0:T(2,128)(2,1)} %dynamic-slice_bitcast_fusion.21), channel_id=1, source_target_pairs={{0,16},{4,20},{8,24},{12,28},{16,0},{20,4},{24,8},{28,12},{1,17},{... | collective-permute-start | bytes 442376 | tf_op jit(solution)/shard_map/ppermute | solution.py:94
  694.3 9.3 %collective-permute-start.24 = (bf16[96,384]{1,0:T(8,128)(2,1)S(1)}, bf16[96,384]{1,0:T(8,128)(2,1)S(1)}, u32[]{:S(2)}, u32[]{:S(2)}) collective-permute-start(bf16[96,384]{1,0:T(8,128)(2,1)S(1)} %bitcast.494), channel_id=1, source_target_pairs={{0,2},{1,3},{2,0},{3,1},{4,6},{5,7},{6,4},{7,5},{8,10},{9,11},{10,... | collective-permute-start | bytes 221192 | tf_op jit(solution)/shard_map/ppermute | solution.py:94
  700.5 35.8 %collective-permute-start.6 = (bf16[2,2,96,2,576]{4,2,3,0,1:T(8,128)(2,1)}, bf16[2,2,96,2,576]{4,2,3,0,1:T(8,128)(2,1)}, u32[]{:S(2)}, u32[]{:S(2)}) collective-permute-start(bf16[2,2,96,2,576]{4,2,3,0,1:T(8,128)(2,1)} %bitcast.413), channel_id=1, source_target_pairs={{0,8},{4,12},{8,0},{12,4},{16,24},{20,28},{24,16},{28,20},{1,9},{5... | collective-permute-start | bytes 2654216 | tf_op jit(solution)/shard_map/ppermute | solution.py:94
  728.3 29.4 %collective-permute-start.31 = (bf16[2,2,2,96,1024]{4,3,0,1,2:T(8,128)(2,1)}, bf16[2,2,2,96,1024]{4,3,0,1,2:T(8,128)(2,1)}, u32[]{:S(2)}, u32[]{:S(2)}) collective-permute-start(bf16[2,2,2,96,1024]{4,3,0,1,2:T(8,128)(2,1)} %bitcast.408), channel_id=1, source_target_pairs={{0,2},{1,3},{2,0},{3,1},{4,6},{5,7},{6,4},{7,5},{8,10},{9,11},{10,... | collective-permute-start | bytes 4718600 | tf_op jit(solution)/shard_map/ppermute | solution.py:94
  734.7 18.3 %collective-permute-start.37 = (bf16[2,256,2,192]{1,0,3,2:T(2,128)(2,1)}, bf16[2,256,2,192]{1,0,3,2:T(2,128)(2,1)}, u32[]{:S(2)}, u32[]{:S(2)}) collective-permute-start(bf16[2,256,2,192]{1,0,3,2:T(2,128)(2,1)} %copy.198), channel_id=1, source_target_pairs={{0,4},{4,0},{8,12},{12,8},{16,20},{20,16},{24,28},{28,24},{1,5},{5... | collective-permute-start | bytes 1179656 | tf_op jit(solution)/shard_map/ppermute | solution.py:94
  739.4 17.2 %collective-permute-start.7 = (bf16[2,96,2,576]{3,1,2,0:T(8,128)(2,1)}, bf16[2,96,2,576]{3,1,2,0:T(8,128)(2,1)}, u32[]{:S(2)}, u32[]{:S(2)}) collective-permute-start(bf16[2,96,2,576]{3,1,2,0:T(8,128)(2,1)} %dynamic-slice_bitcast_fusion.7), channel_id=1, source_target_pairs={{0,4},{4,0},{8,12},{12,8},{16,20},{20,16},{24,28},{28,24},{1,5},{5... | collective-permute-start | bytes 1327112 | tf_op jit(solution)/shard_map/ppermute | solution.py:94
  755.4 8.7 %collective-permute-start.38 = (bf16[256,2,192]{0,2,1:T(8,128)(2,1)S(1)}, bf16[256,2,192]{0,2,1:T(8,128)(2,1)S(1)}, u32[]{:S(2)}, u32[]{:S(2)}) collective-permute-start(bf16[256,2,192]{0,2,1:T(8,128)(2,1)S(1)} %bitcast.493), channel_id=1, source_target_pairs={{0,16},{4,20},{8,24},{12,28},{16,0},{20,4},{24,8},{28,12},{1,17},{... | collective-permute-start | bytes 589832 | tf_op jit(solution)/shard_map/ppermute | solution.py:94
  760.1 12.2 %collective-permute-start.32 = (bf16[2,2,96,1024]{3,2,0,1:T(8,128)(2,1)S(1)}, bf16[2,2,96,1024]{3,2,0,1:T(8,128)(2,1)S(1)}, u32[]{:S(2)}, u32[]{:S(2)}) collective-permute-start(bf16[2,2,96,1024]{3,2,0,1:T(8,128)(2,1)S(1)} %dynamic-slice_bitcast_fusion.5), channel_id=1, source_target_pairs={{0,4},{4,0},{8,12},{12,8},{16,20},{20,16},{24,28},{28,24},{1,5},{5... | collective-permute-start | bytes 2359304 | tf_op jit(solution)/shard_map/ppermute | solution.py:94
  761.7 9.5 %collective-permute-start.8 = (bf16[96,2,576]{2,0,1:T(8,128)(2,1)S(1)}, bf16[96,2,576]{2,0,1:T(8,128)(2,1)S(1)}, u32[]{:S(2)}, u32[]{:S(2)}) collective-permute-start(bf16[96,2,576]{2,0,1:T(8,128)(2,1)S(1)} %dynamic-slice_bitcast_fusion.16), channel_id=1, source_target_pairs={{0,16},{4,20},{8,24},{12,28},{16,0},{20,4},{24,8},{28,12},{1,17},{... | collective-permute-start | bytes 663560 | tf_op jit(solution)/shard_map/ppermute | solution.py:94
  764.3 9.9 %collective-permute-start.39 = (bf16[256,192]{0,1:T(8,128)(2,1)S(1)}, bf16[256,192]{0,1:T(8,128)(2,1)S(1)}, u32[]{:S(2)}, u32[]{:S(2)}) collective-permute-start(bf16[256,192]{0,1:T(8,128)(2,1)S(1)} %dynamic-slice_bitcast_fusion.23), channel_id=1, source_target_pairs={{0,2},{1,3},{2,0},{3,1},{4,6},{5,7},{6,4},{7,5},{8,10},{9,11},{10,... | collective-permute-start | bytes 294920 | tf_op jit(solution)/shard_map/ppermute | solution.py:94
  771.3 4.9 collective-permute-start.9
  772.6 8.9 %collective-permute-start.33 = (bf16[2,96,1024]{2,1,0:T(8,128)(2,1)S(1)}, bf16[2,96,1024]{2,1,0:T(8,128)(2,1)S(1)}, u32[]{:S(2)}, u32[]{:S(2)}) collective-permute-start(bf16[2,96,1024]{2,1,0:T(8,128)(2,1)S(1)} %dynamic-slice_bitcast_fusion.8), channel_id=1, source_target_pairs={{0,8},{4,12},{8,0},{12,4},{16,24},{20,28},{24,16},{28,20},{1,9},{5... | collective-permute-start | bytes 1179656 | tf_op jit(solution)/shard_map/ppermute | solution.py:94
  781.7 8.7 %collective-permute-start.34 = (bf16[96,1024]{1,0:T(8,128)(2,1)S(1)}, bf16[96,1024]{1,0:T(8,128)(2,1)S(1)}, u32[]{:S(2)}, u32[]{:S(2)}) collective-permute-start(bf16[96,1024]{1,0:T(8,128)(2,1)S(1)} %dynamic-slice_bitcast_fusion.17), channel_id=1, source_target_pairs={{0,16},{4,20},{8,24},{12,28},{16,0},{20,4},{24,8},{28,12},{1,17},{... | collective-permute-start | bytes 589832 | tf_op jit(solution)/shard_map/ppermute | solution.py:94
  (78 other events, 282.0 us)

commit v2 on v1

v2 whole, which is shorter than its diff:
```python
import jax
import jax.numpy as jnp
from jax import lax
from jax.experimental import pallas as pl
from jax.experimental.pallas import tpu as pltpu
from jax.sharding import PartitionSpec as P

HD = 64
LANES = 128
BLOCKS = 8

eps = 1e-06
neg_big = -1e30
gelu_scale = 0.7978845608028654
gelu_cubic = 0.044715
low = jnp.bfloat16
high = jnp.float32
vmem_bytes = 60 * 1024 * 1024


def rows_dot(left_side, right_side):
    return lax.dot_general(
        left_side, right_side, (((1,), (1,)), ((), ())), preferred_element_type=high
    )


def cols_dot(left_side, right_side):
    return lax.dot_general(
        left_side, right_side, (((0,), (0,)), ((), ())), preferred_element_type=high
    )


def plain_dot(left_side, right_side):
    return jnp.dot(left_side, right_side, preferred_element_type=high)


def inverse_scale(hidden):
    return lax.rsqrt(jnp.mean(hidden * hidden, axis=-1, keepdims=True) + eps)


def norm_back(hidden, gain, grad):
    scale = inverse_scale(hidden)
    weighted = gain * grad
    middle = jnp.mean(weighted * hidden, axis=-1, keepdims=True)
    to_rows = scale * (weighted - hidden * (scale * scale * middle))
    to_gain = jnp.sum(grad * hidden * scale, axis=0, keepdims=True)
    return to_rows, to_gain


def cost(products, moved, powers=0):
    return pl.CostEstimate(flops=2 * products, bytes_accessed=moved, transcendentals=powers)


def size_of(*pieces):
    return sum(piece.size * piece.dtype.itemsize for piece in pieces)


def after(piece, *earlier):
    return lax.optimization_barrier((piece, *earlier))[0]


def row_spec(rows, width):
    return pl.BlockSpec((rows, width), lambda step: (step, 0))


def whole_spec(shape):
    return pl.BlockSpec(
        shape, lambda step: (0,) * len(shape), pipeline_mode=pl.Buffered(1)
    )


def row_call(kernel, name, step_rows, by_rows, constants, outs, sums=(), passes=2):
    total = by_rows[0].shape[0]
    step_rows = min(step_rows, total)
    return pl.pallas_call(
        kernel,
        grid=(total // step_rows,),
        in_specs=[row_spec(step_rows, piece.shape[1]) for piece in by_rows]
        + [whole_spec(piece.shape) for piece in constants],
        out_specs=[row_spec(step_rows, width) for width, _ in outs]
        + [pl.BlockSpec((1, width), lambda step: (0, 0)) for width in sums],
        out_shape=[jax.ShapeDtypeStruct((total, width), kind) for width, kind in outs]
        + [jax.ShapeDtypeStruct((1, width), high) for width in sums],
        cost_estimate=cost(
            total * sum(piece.size for piece in constants) * passes, size_of(*by_rows, *constants)
        ),
        compiler_params=pltpu.CompilerParams(vmem_limit_bytes=vmem_bytes),
        name=name,
    )(*by_rows, *constants)


def add_up(total_ref, part):
    @pl.when(pl.program_id(0) == 0)
    def _():
        total_ref[...] = jnp.zeros_like(total_ref)

    total_ref[...] += part


def enter_self(tokens_ref, gain_ref, wq_ref, wk_ref, wv_ref, normed_ref, q_ref, k_ref, v_ref):
    hidden = tokens_ref[...].astype(high)
    normed = (hidden * inverse_scale(hidden) * gain_ref[...]).astype(low)
    normed_ref[...] = normed
    q_ref[...] = plain_dot(normed, wq_ref[...]).astype(low)
    k_ref[...] = plain_dot(normed, wk_ref[...]).astype(low)
    v_ref[...] = plain_dot(normed, wv_ref[...]).astype(low)


def enter_memory(memory_ref, wk_ref, wv_ref, k_ref, v_ref):
    rows = memory_ref[...]
    k_ref[...] = plain_dot(rows, wk_ref[...]).astype(low)
    v_ref[...] = plain_dot(rows, wv_ref[...]).astype(low)


def enter_cross(attended_ref, tokens_ref, gain_ref, out_ref, wq_ref, hidden_ref, normed_ref, q_ref):
    hidden = tokens_ref[...].astype(high) + plain_dot(attended_ref[...], out_ref[...])
    hidden_ref[...] = hidden
    normed = (hidden * inverse_scale(hidden) * gain_ref[...]).astype(low)
    normed_ref[...] = normed
    q_ref[...] = plain_dot(normed, wq_ref[...]).astype(low)


def feed_both(
    crossed_ref,
    hidden_ref,
    cotangent_ref,
    gain_ref,
    out_ref,
    gate_ref,
    up_ref,
    down_ref,
    normed_ref,
    mixed_ref,
    grad_gate_ref,
    grad_up_ref,
    result_ref,
    grad_hidden_ref,
    branch_ref,
    grad_crossed_ref,
    grad_gain_ref,
):
    gain = gain_ref[...]
    hidden = hidden_ref[...] + plain_dot(crossed_ref[...], out_ref[...])
    normed = (hidden * inverse_scale(hidden) * gain).astype(low)
    normed_ref[...] = normed
    gate = plain_dot(normed, gate_ref[...])
    up = plain_dot(normed, up_ref[...])
    square = gate * gate
    curve = jnp.tanh(gelu_scale * (gate + gelu_cubic * gate * square))
    half = 0.5 * (1.0 + curve)
    bent = gate * half
    slope = half + 0.5 * gate * (1.0 - curve * curve) * (
        gelu_scale * (1.0 + 3.0 * gelu_cubic * square)
    )
    mixed = (bent * up).astype(low)
    mixed_ref[...] = mixed
    result_ref[...] = (hidden + plain_dot(mixed, down_ref[...])).astype(low)
    cotangent = cotangent_ref[...]
    back = rows_dot(cotangent, down_ref[...])
    grad_gate = (back * up * slope).astype(low)
    grad_up = (back * bent).astype(low)
    grad_gate_ref[...] = grad_gate
    grad_up_ref[...] = grad_up
    grad_normed = rows_dot(grad_gate, gate_ref[...]) + rows_dot(grad_up, up_ref[...])
    to_rows, to_gain = norm_back(hidden, gain, grad_normed)
    grad_hidden = cotangent.astype(high) + to_rows
    grad_hidden_ref[...] = grad_hidden
    branch = grad_hidden.astype(low)
    branch_ref[...] = branch
    grad_crossed_ref[...] = rows_dot(branch, out_ref[...]).astype(low)
    add_up(grad_gain_ref, to_gain)


def leave_cross(
    grad_q_ref,
    hidden_ref,
    grad_in_ref,
    gain_ref,
    wq_ref,
    out_ref,
    grad_hidden_ref,
    branch_ref,
    grad_attended_ref,
    grad_gain_ref,
):
    to_rows, to_gain = norm_back(
        hidden_ref[...], gain_ref[...], rows_dot(grad_q_ref[...], wq_ref[...])
    )
    grad_hidden = grad_in_ref[...] + to_rows
    grad_hidden_ref[...] = grad_hidden
    branch = grad_hidden.astype(low)
    branch_ref[...] = branch
    grad_attended_ref[...] = rows_dot(branch, out_ref[...]).astype(low)
    add_up(grad_gain_ref, to_gain)


def leave_memory(grad_k_ref, grad_v_ref, wk_ref, wv_ref, grad_ref):
    grad_ref[...] = (
        rows_dot(grad_k_ref[...], wk_ref[...]) + rows_dot(grad_v_ref[...], wv_ref[...])
    ).astype(low)


def leave_self(
    grad_q_ref,
    grad_k_ref,
    grad_v_ref,
    tokens_ref,
    grad_in_ref,
    gain_ref,
    wq_ref,
    wk_ref,
    wv_ref,
    grad_ref,
    grad_gain_ref,
):
    grad_normed = (
        rows_dot(grad_q_ref[...], wq_ref[...])
        + rows_dot(grad_k_ref[...], wk_ref[...])
        + rows_dot(grad_v_ref[...], wv_ref[...])
    )
    to_rows, to_gain = norm_back(tokens_ref[...].astype(high), gain_ref[...], grad_normed)
    grad_ref[...] = (grad_in_ref[...] + to_rows).astype(low)
    add_up(grad_gain_ref, to_gain)


def two_heads(rows):
    first = lax.broadcasted_iota(jnp.int32, rows.shape, 1) < HD
    zero = jnp.zeros_like(rows)
    return jnp.concatenate([jnp.where(first, rows, zero), jnp.where(first, zero, rows)], axis=0)


def one_pair(stacked):
    half = stacked.shape[1] // 2
    first = lax.broadcasted_iota(jnp.int32, (stacked.shape[0], half), 0) < HD
    return jnp.where(first, stacked[:, :half], stacked[:, half:]).T


def attend_forward_kernel(
    causal, step, count_ref, q_ref, k_ref, v_ref, weight_ref, mixed_ref, inverse_ref, score_ref
):
    queries = two_heads(q_ref[...])
    wide = queries.shape[0]
    peak = jnp.full((1, wide), neg_big, high)
    for begin in range(0, k_ref.shape[0], step):
        here = slice(begin, begin + step)
        scores = rows_dot(k_ref[here, :], queries)
        if causal:
            key = lax.broadcasted_iota(jnp.int32, (step, wide), 0) + begin
            token = lax.broadcasted_iota(jnp.int32, (step, wide), 1)
            token = jnp.where(token >= wide // 2, token - wide // 2, token)
            scores = jnp.where(key <= token, scores, neg_big)
        else:
            key = lax.broadcasted_iota(jnp.int32, (step, 1), 0) + begin
            scores = scores + jnp.where(key < count_ref[0], 0.0, neg_big)
        score_ref[here, :] = scores
        peak = jnp.maximum(peak, jnp.max(scores, axis=0, keepdims=True))
    total = jnp.zeros((1, wide), high)
    mixed = jnp.zeros((q_ref.shape[1], wide), high)
    for begin in range(0, k_ref.shape[0], step):
        here = slice(begin, begin + step)
        weights = jnp.exp(score_ref[here, :] - peak)
        total = total + jnp.sum(weights, axis=0, keepdims=True)
        weights = weights.astype(low)
        weight_ref[0, here, :] = weights
        mixed = mixed + cols_dot(v_ref[here, :], weights)
    inverse = 1.0 / total
    inverse_ref[0] = inverse
    mixed_ref[...] = one_pair(mixed * inverse).astype(low)


def attend_forward(queries, keys, values, count, causal, step, name):
    tokens, width = queries.shape
    patches = keys.shape[0]
    pairs = width // LANES
    by_pair = lambda rows: pl.BlockSpec((rows, LANES), lambda pair, _: (0, pair))
    return pl.pallas_call(
        lambda *refs: attend_forward_kernel(causal, step, *refs),
        out_shape=(
            jax.ShapeDtypeStruct((pairs, patches, 2 * tokens), low),
            jax.ShapeDtypeStruct((tokens, width), low),
            jax.ShapeDtypeStruct((pairs, 1, 2 * tokens), high),
        ),
        grid_spec=pltpu.PrefetchScalarGridSpec(
            num_scalar_prefetch=1,
            grid=(pairs,),
            in_specs=[by_pair(tokens), by_pair(patches), by_pair(patches)],
            out_specs=[
                pl.BlockSpec((1, patches, 2 * tokens), lambda pair, _: (pair, 0, 0)),
                by_pair(tokens),
                pl.BlockSpec((1, 1, 2 * tokens), lambda pair, _: (pair, 0, 0)),
            ],
            scratch_shapes=[pltpu.VMEM((patches, 2 * tokens), high)],
        ),
        cost_estimate=cost(8 * patches * tokens * width, size_of(queries, keys, values)),
        compiler_params=pltpu.CompilerParams(vmem_limit_bytes=vmem_bytes),
        name=name,
    )(count, queries, keys, values)


def attend_backward_kernel(
    step,
    weight_ref,
    inverse_ref,
    q_ref,
    k_ref,
    v_ref,
    mixed_ref,
    grad_mixed_ref,
    *out_refs,
):
    grad_q_ref, grad_k_ref, grad_v_ref = out_refs[-3:]
    queries = two_heads(q_ref[...])
    grads = grad_mixed_ref[...].astype(high).T
    mixed = mixed_ref[...].astype(high).T
    first = lax.broadcasted_iota(jnp.int32, grads.shape, 0) < HD
    zero = jnp.zeros_like(grads)
    scaled = jnp.concatenate(
        [jnp.where(first, grads, zero), jnp.where(first, zero, grads)], axis=1
    )
    scaled = (scaled * inverse_ref[0]).astype(low)
    wide = scaled.astype(high)
    centre = jnp.sum(wide * jnp.concatenate([mixed, mixed], axis=1), axis=0, keepdims=True)
    rows = wide.T.astype(low)
    grad_q = jnp.zeros(wide.shape, high)
    for begin in range(0, k_ref.shape[0], step):
        here = slice(begin, begin + step)
        weights = weight_ref[0, here, :]
        grad_probs = plain_dot(v_ref[here, :], scaled)
        grad_scores = (weights.astype(high) * (grad_probs - centre)).astype(low)
        grad_v_ref[here, :] = plain_dot(weights, rows).astype(low)
        grad_k_ref[here, :] = plain_dot(grad_scores, queries).astype(low)
        grad_q = grad_q + cols_dot(k_ref[here, :], grad_scores)
    grad_q_ref[...] = one_pair(grad_q).astype(low)


def attend_backward(weights, inverse, queries, keys, values, mixed, grad_mixed, step, name, first, end, filled=()):
    tokens, width = queries.shape
    patches = keys.shape[0]
    by_token = pl.BlockSpec((tokens, LANES), lambda pair: (0, pair + first))
    by_patch = pl.BlockSpec((patches, LANES), lambda pair: (0, pair + first))
    return pl.pallas_call(
        lambda *refs: attend_backward_kernel(step, *refs),
        out_shape=(
            jax.ShapeDtypeStruct((tokens, width), low),
            jax.ShapeDtypeStruct((patches, width), low),
            jax.ShapeDtypeStruct((patches, width), low),
        ),
        grid=(end - first,),
        in_specs=[
            pl.BlockSpec((1, patches, 2 * tokens), lambda pair: (pair + first, 0, 0)),
            pl.BlockSpec((1, 1, 2 * tokens), lambda pair: (pair + first, 0, 0)),
            by_token,
            by_patch,
            by_patch,
            by_token,
            by_token,
        ]
        + [pl.BlockSpec(memory_space=pl.ANY)] * len(filled),
        out_specs=[by_token, by_patch, by_patch],
        input_output_aliases={7 + which: which for which in range(len(filled))},
        cost_estimate=cost(
            12 * patches * tokens * LANES * (end - first), 4 * patches * tokens * (end - first)
        ),
        compiler_params=pltpu.CompilerParams(vmem_limit_bytes=vmem_bytes),
        name=name,
    )(weights, inverse, queries, keys, values, mixed, grad_mixed, *filled)


def swap(piece, axis_name, bit):
    size = lax.axis_size(axis_name)
    return lax.ppermute(piece, axis_name, [(place, place ^ (1 << bit)) for place in range(size)])


def bit_of(axis_name, bit):
    return (lax.axis_index(axis_name) >> bit) & 1


def pick(piece, which):
    return lax.dynamic_index_in_dim(piece, which, 0, keepdims=False)


class Parcel:
    def __init__(self, order, parts, shapes, extra=0):
        self.order = order
        self.parts = parts
        self.plain = [shapes[job][1] // 4 // LANES for job, _, _ in parts]
        self.mixed = [int(shapes[job][1] // 4 % LANES > 0) for job, _, _ in parts]
        heights = [end - begin for _, begin, end in parts]
        self.own = sum(tiles * height for tiles, height in zip(self.plain, heights))
        self.extra = extra
        self.both = extra + sum(tiles * height for tiles, height in zip(self.mixed, heights))
        self.rows = 2 * self.own + self.both
        at, both_at = 0, 0
        self.at, self.both_at = [], []
        for tiles, shared, height in zip(self.plain, self.mixed, heights):
            self.at.append(at)
            self.both_at.append(both_at)
            at += tiles * height
            both_at += shared * height

    def place(self, block):
        bits = [(block >> bit) & 1 for bit in self.order]
        return bits[0] * 4 + bits[1] * 2 + bits[2]


def core_tiles(grad, core):
    quarter = grad.shape[1] // 4
    starts = [core * quarter, 2 * quarter + core * quarter]
    tiles = [
        grad[:, start + at : start + at + LANES]
        for start in starts
        for at in range(0, quarter - LANES + 1, LANES)
    ]
    rest = quarter % LANES
    if rest:
        tiles.append(
            jnp.concatenate(
                [grad[:, start + quarter - rest : start + quarter] for start in starts], axis=1
            )
        )
    return tiles


def weight_kernel(jobs, parcels, n_in, core_ref, *refs):
    ins, outs, turned_ref = refs[:n_in], refs[n_in:-1], refs[-1]
    core = core_ref[0]
    for which, parcel in enumerate(parcels):
        if parcel.extra:
            for kind in (0, 1):
                for block in range(BLOCKS):
                    outs[2 * which + kind][block, parcel.rows - parcel.extra :, :] = ins[-1][...]
    last_rows = None
    for job, (row_at, grad_at) in enumerate(jobs):
        rows_ref, grad = ins[row_at], ins[grad_at][...]
        depth, height = rows_ref.shape
        if row_at != last_rows:
            turned_ref[:height, :depth] = rows_ref[...].T
            last_rows = row_at
        turned = turned_ref[:height, :depth]
        sides = [core_tiles(grad, 0), core_tiles(grad, 1)]
        count = len(sides[0])
        wanted = [
            (kind, tile, jnp.where(core == kind, sides[0][tile], sides[1][tile]))
            for kind in (0, 1)
            for tile in range(count)
        ]
        for begin in range(0, 2 * count, 2):
            group = wanted[begin : begin + 2]
            product = plain_dot(turned, jnp.concatenate([piece for _, _, piece in group], axis=1))
            product = product.astype(low)
            block_rows = height // BLOCKS
            for slot, (kind, tile, _) in enumerate(group):
                for which, parcel in enumerate(parcels):
                    for part, (owner, first, end) in enumerate(parcel.parts):
                        if owner != job:
                            continue
                        plain = parcel.plain[part]
                        span = end - first
                        if tile < 2 * plain:
                            at = (tile // plain) * parcel.own + parcel.at[part] + (tile % plain) * span
                        else:
                            at = 2 * parcel.own + parcel.both_at[part]
                        for block in range(BLOCKS):
                            top = block * block_rows
                            outs[2 * which + kind][parcel.place(block), at : at + span, :] = product[
                                top + first : top + end, slot * LANES : (slot + 1) * LANES
                            ]


def weight_parts(core, arrays, jobs, parcels, name):
    depth = max(arrays[row_at].shape[0] for row_at, _ in jobs)
    height = max(arrays[row_at].shape[1] for row_at, _ in jobs)
    vmem = pl.BlockSpec(memory_space=pltpu.VMEM)
    return pl.pallas_call(
        lambda *refs: weight_kernel(jobs, parcels, len(arrays), *refs),
        in_specs=[pl.BlockSpec(memory_space=pltpu.SMEM)] + [vmem] * len(arrays),
        out_specs=[vmem] * (2 * len(parcels)),
        out_shape=[
            jax.ShapeDtypeStruct((BLOCKS, parcel.rows, LANES), low)
            for parcel in parcels
            for _ in range(2)
        ],
        scratch_shapes=[pltpu.VMEM((height, depth), low)],
        cost_estimate=cost(
            sum(arrays[row_at].size * arrays[grad_at].shape[1] for row_at, grad_at in jobs) * 2,
            size_of(*arrays),
        ),
        compiler_params=pltpu.CompilerParams(vmem_limit_bytes=vmem_bytes),
        name=name,
    )(core, *arrays)


class Travel:
    def __init__(self, parcel, kept, sent):
        self.parcel = parcel
        self.kept = kept
        self.received = swap(sent, "narrow", 0)
        self.bits = list(parcel.order)

    def step(self, *earlier):
        parcel = self.parcel
        kept, received = self.kept, self.received
        if earlier:
            kept, received = lax.optimization_barrier((kept, received, *earlier))[:2]
        if self.bits:
            top = lax.axis_size("items").bit_length() - 4
            bit = self.bits.pop(0)
            mine = bit_of("items", top + bit)
            half = kept.shape[0] // 2
            kept = kept.reshape(2, half, parcel.rows, LANES)
            received = received.reshape(2, half, parcel.rows, LANES)
            both = lambda which: (
                pick(kept, which).astype(high) + pick(received, which).astype(high)
            ).astype(low)
            away, self.kept = both(1 - mine), both(mine)
            self.received = swap(away, "items", top + bit)
        else:
            total = (kept[0].astype(high) + received[0].astype(high)).astype(low)
            mine = bit_of("narrow", 1)
            shared = total[2 * parcel.own :]

            def side(which):
                own = lax.dynamic_slice_in_dim(total, which * parcel.own, parcel.own, 0)
                return jnp.concatenate([own, shared], axis=0) if parcel.both else own

            away, self.kept = side(1 - mine), side(mine)
            self.received = swap(away, "narrow", 1)
        return self.kept, away


def finish_kernel(parcels, x_ref, *refs):
    x = x_ref[0]
    outs = refs[2 * len(parcels) :]
    for which, parcel in enumerate(parcels):
        total = refs[2 * which][...].astype(high) + refs[2 * which + 1][...].astype(high)
        for part, (job, first, end) in enumerate(parcel.parts):
            span = end - first
            for tile in range(parcel.plain[part]):
                at = parcel.at[part] + tile * span
                outs[job][first:end, tile * LANES : (tile + 1) * LANES] = total[at : at + span]
            if parcel.mixed[part]:
                at = parcel.own + parcel.both_at[part]
                shared = total[at : at + span]
                half = LANES // 2
                begin = parcel.plain[part] * LANES
                outs[job][first:end, begin : begin + half] = jnp.where(
                    x == 0, shared[:, :half], shared[:, half:]
                )
        if parcel.extra:
            outs[-1][...] = total[-parcel.extra :]


def start_weights(arrays, jobs, parcels, name):
    pieces = weight_parts(bit_of("narrow", 0).reshape(1), arrays, jobs, parcels, name)
    return [
        Travel(parcel, pieces[2 * which], pieces[2 * which + 1])
        for which, parcel in enumerate(parcels)
    ]


def end_weights(travels, shapes, name):
    parcels = [trip.parcel for trip in travels]
    ends = [piece for trip in travels for piece in (trip.kept, trip.received)]
    vmem = pl.BlockSpec(memory_space=pltpu.VMEM)
    extra = sum(parcel.extra for parcel in parcels)
    out_shapes = [(height // BLOCKS, width // 4) for height, width in shapes]
    out_shapes += [(extra, LANES)] if extra else []
    outs = pl.pallas_call(
        lambda *refs: finish_kernel(parcels, *refs),
        in_specs=[pl.BlockSpec(memory_space=pltpu.SMEM)] + [vmem] * len(ends),
        out_specs=[vmem] * len(out_shapes),
        out_shape=[jax.ShapeDtypeStruct(shape, high) for shape in out_shapes],
        compiler_params=pltpu.CompilerParams(vmem_limit_bytes=vmem_bytes),
        name=name,
    )(bit_of("narrow", 1).reshape(1), *ends)
    sums, extras = list(outs[: len(shapes)]), list(outs[len(shapes) :])
    levels = lax.axis_size("items").bit_length() - 1
    for bit in range(levels - 4, -1, -1):
        mine = bit_of("items", bit)
        halves = [piece.reshape(2, piece.shape[0] // 2, piece.shape[1]) for piece in sums]
        sums = [pick(piece, mine) + swap(pick(piece, 1 - mine), "items", bit) for piece in halves]
        extras = [piece + swap(piece, "items", bit) for piece in extras]
    return sums + extras


def exchange(piece):
    return lax.all_to_all(piece, "narrow", split_axis=0, concat_axis=0, tiled=True)


def body(
    tokens,
    memory,
    mem_count,
    cotangent,
    gain_self,
    self_query,
    self_key,
    self_value,
    self_out,
    gain_cross,
    cross_query,
    cross_key,
    cross_value,
    cross_out,
    gain_feed,
    gate_weight,
    up_weight,
    down_weight,
):
    width = tokens.shape[2]
    inner = gate_weight.shape[1]
    gain_self, gain_cross, gain_feed = [
        gain.reshape(1, width) for gain in (gain_self, gain_cross, gain_feed)
    ]
    token_rows = exchange(tokens).reshape(-1, width)
    memory_rows = exchange(memory).reshape(-1, width)
    cotangent_rows = exchange(cotangent).reshape(-1, width)
    count = pick(mem_count, lax.axis_index("narrow")).reshape(1)
    normed_one, query_one, key_one, value_one = row_call(
        enter_self,
        "enter_self",
        256,
        [token_rows],
        [gain_self, self_query, self_key, self_value],
        [(width, low)] * 4,
    )
    weights_one, attended, inverse_one = attend_forward(
        query_one, key_one, value_one, count, True, 256, "self_forward"
    )
    hidden_one, normed_two, query_two = row_call(
        enter_cross,
        "enter_cross",
        256,
        [attended, token_rows],
        [gain_cross, self_out, cross_query],
        [(width, high), (width, low), (width, low)],
    )
    memory_keys, memory_values = row_call(
        enter_memory,
        "enter_memory",
        512,
        [memory_rows],
        [cross_key, cross_value],
        [(width, low)] * 2,
    )
    weights_two, crossed, inverse_two = attend_forward(
        query_two, memory_keys, memory_values, count, False, 512, "cross_forward"
    )
    (
        normed_three,
        mixed,
        grad_gate,
        grad_up,
        result,
        grad_hidden_two,
        branch_two,
        grad_crossed,
        grad_gain_feed,
    ) = row_call(
        feed_both,
        "feed_both",
        256,
        [crossed, hidden_one, cotangent_rows],
        [gain_feed, cross_out, gate_weight, up_weight, down_weight],
        [
            (width, low),
            (inner, low),
            (inner, low),
            (inner, low),
            (width, low),
            (width, high),
            (width, low),
            (width, low),
        ],
        [width],
    )
    square = (width, width)
    feed_shapes = [(width, inner), (width, inner), (inner, width), square]
    rows, tall = width // BLOCKS, inner // BLOCKS
    feed_trips = start_weights(
        [normed_three, grad_gate, grad_up, mixed, cotangent_rows, crossed, branch_two],
        [(0, 1), (0, 2), (3, 4), (5, 6)],
        [
            Parcel((0, 1, 2), [(0, 0, rows), (2, 0, tall // 2)], feed_shapes),
            Parcel((1, 0, 2), [(1, 0, rows), (2, tall // 2, tall), (3, 0, rows)], feed_shapes),
        ],
        "feed_weights",
    )
    result = exchange(result.reshape(tokens.shape))
    step = lambda trips, earlier: [part for trip in trips for part in trip.step(earlier)]
    ready = feed_trips[0].kept
    grads_two = ()
    for first in (0, 2, 4):
        grads_two = attend_backward(
            weights_two,
            inverse_two,
            query_two,
            memory_keys,
            memory_values,
            crossed,
            after(grad_crossed, ready),
            512,
            "cross_backward",
            first,
            first + 2,
            grads_two,
        )
        ready = step(feed_trips, grads_two[0])[0]
    grad_query_two, memory_keys_grad, memory_values_grad = grads_two
    grad_hidden_one, branch_one, grad_attended, grad_gain_cross = row_call(
        leave_cross,
        "leave_cross",
        256,
        [after(grad_query_two, ready), hidden_one, grad_hidden_two],
        [gain_cross, cross_query, self_out],
        [(width, high), (width, low), (width, low)],
        [width],
    )
    (memory_grad,) = row_call(
        leave_memory,
        "leave_memory",
        512,
        [after(memory_keys_grad, branch_one), memory_values_grad],
        [cross_key, cross_value],
        [(width, low)],
        passes=1,
    )
    ready = step(feed_trips, memory_grad)[0]
    memory_grad = exchange(memory_grad.reshape(memory.shape)).astype(high)
    cross_shapes = [square] * 4
    cross_trips = start_weights(
        [
            memory_rows,
            after(memory_keys_grad, ready),
            memory_values_grad,
            normed_two,
            grad_query_two,
            attended,
            branch_one,
        ],
        [(0, 1), (0, 2), (3, 4), (5, 6)],
        [
            Parcel((0, 1, 2), [(0, 0, rows), (2, 0, rows)], cross_shapes),
            Parcel((1, 0, 2), [(1, 0, rows), (3, 0, rows)], cross_shapes),
        ],
        "cross_weights",
    )
    ready = cross_trips[0].kept
    grads_one = ()
    for first in (0, 3):
        grads_one = attend_backward(
            weights_one,
            inverse_one,
            query_one,
            key_one,
            value_one,
            attended,
            after(grad_attended, ready),
            512,
            "self_backward",
            first,
            first + 3,
            grads_one,
        )
        ready = step(cross_trips, grads_one[0])[0]
    grad_query_one, key_one_grad, value_one_grad = grads_one
    tokens_grad, grad_gain_self = row_call(
        leave_self,
        "leave_self",
        256,
        [after(grad_query_one, ready), key_one_grad, value_one_grad, token_rows, grad_hidden_one],
        [gain_self, self_query, self_key, self_value],
        [(width, low)],
        [width],
    )
    gains = jnp.concatenate([grad_gain_self, grad_gain_cross, grad_gain_feed], axis=0).astype(low)
    gains = jnp.pad(gains.reshape(-1, LANES), ((0, 32 - 3 * width // LANES), (0, 0)))
    self_shapes = [square] * 3
    self_trips = start_weights(
        [normed_one, grad_query_one, key_one_grad, value_one_grad, gains],
        [(0, 1), (0, 2), (0, 3)],
        [
            Parcel((0, 1, 2), [(0, 0, rows), (2, 0, rows // 2)], self_shapes, 32),
            Parcel((1, 0, 2), [(1, 0, rows), (2, rows // 2, rows)], self_shapes),
        ],
        "self_weights",
    )
    tokens_grad = exchange(tokens_grad.reshape(tokens.shape)).astype(high)
    gate_sum, up_sum, down_sum, cross_out_sum = end_weights(
        feed_trips, feed_shapes, "feed_weights_end"
    )
    for trip in self_trips + cross_trips:
        trip.step()
    for trip in self_trips + cross_trips:
        trip.step()
    for trip in self_trips:
        trip.step()
    for trip in self_trips:
        trip.step()
    cross_key_sum, cross_value_sum, cross_query_sum, self_out_sum = end_weights(
        cross_trips, cross_shapes, "cross_weights_end"
    )
    self_query_sum, self_key_sum, self_value_sum, gains = end_weights(
        self_trips, self_shapes, "self_weights_end"
    )
    gains = gains[: 3 * width // LANES].reshape(3, width)
    return (
        result,
        tokens_grad,
        memory_grad,
        gains[0],
        self_query_sum,
        self_key_sum,
        self_value_sum,
        self_out_sum,
        gains[1],
        cross_query_sum,
        cross_key_sum,
        cross_value_sum,
        cross_out_sum,
        gains[2],
        gate_sum,
        up_sum,
        down_sum,
    )


def solution(mesh):
    in_specs = (
        P("items", "narrow", None),
        P("items", "narrow", None),
        P("items"),
        P("items", "narrow", None),
        P(),
        P(),
        P(),
        P(),
        P(),
        P(),
        P(),
        P(),
        P(),
        P(),
        P(),
        P(),
        P(),
        P(),
    )
    out_specs = (
        P("items", "narrow", None),
        P("items", "narrow", None),
        P("items", "narrow", None),
        P(),
        P("items", "narrow"),
        P("items", "narrow"),
        P("items", "narrow"),
        P("items", "narrow"),
        P(),
        P("items", "narrow"),
        P("items", "narrow"),
        P("items", "narrow"),
        P("items", "narrow"),
        P(),
        P("items", "narrow"),
        P("items", "narrow"),
        P("items", "narrow"),
    )
    return jax.shard_map(body, mesh=mesh, in_specs=in_specs, out_specs=out_specs, check_vma=False)
```

time: 801 us -> 390 us (0.49)
  matrix products: 274 us -> 0 us
  Pallas kernels: 0 us -> 186 us
  local copies, waits for them, and re-layouts: 193 us -> 13.2 us
  other arithmetic: 164 us -> 41.5 us
  starting transfers between devices: 71.3 us -> 53.5 us
  blocking collectives: 0 us -> 16.5 us
  waiting for transfers between devices: 87.2 us -> 73.6 us
    dot_general x48 -> x0, matrix products: 274 us -> none  [the longest x14 47.3 us: outer_rows(): lax.dot_general(left_side, right_side, (((0,), (0,)), ((), ())), preferre...]
    pallas_call x0 -> x20, Pallas kernels: none -> 186 us  [the longest x7 63.5 us: row_call(): pl.pallas_call(kernel, grid=(total // step_rows,), in_specs=[row_spec(ste...]
    unnamed x4 -> x0, other arithmetic: 47.9 us -> none
    unnamed x208 -> x38, local copies, waits for them, and re-layouts: 52.6 us -> 7.93 us
    dynamic_slice x15 -> x6, local copies, waits for them, and re-layouts: 41.2 us -> 1.54 us  [the longest x5 0.96 us: side(): own = lax.dynamic_slice_in_dim(total, which * parcel.own, parcel.own, 0)]
    convert_element_type x30 -> x26, other arithmetic: 74.7 us -> 36.5 us  [the longest x18 27.8 us: step(): both = lambda which: (pick(kept, which).astype(high) + pick(received, whi...]
    reshape x12 -> x3, local copies, waits for them, and re-layouts: 37.8 us -> 1.74 us  [body(): gain.reshape(1, width)]
    reduce_sum x3 -> x0, other arithmetic: 24.3 us -> none  [the longest x2 22.9 us: attend_forward(): row_total = jnp.sum(exp_scores, axis=-1, keepdims=True)]
  transfers between devices with their start and end apart: 46 -> 35, of which waited for: 18 -> 11; matrix products, arithmetic and copies ran while one was open for 40% -> 11% of each run, Pallas kernels for 0% -> 39%
where the time goes in v2:
time: 390 us; the launch traced here: 386 us
  Pallas kernels  186 us (48%)
  waiting for transfers between devices  73.6 us (19%)
  starting transfers between devices  53.5 us (14%)
  other arithmetic  41.5 us (11%)
  blocking collectives  16.5 us (4%)
  local copies, waits for them, and re-layouts  13.2 us (3%)
    pallas_call x7, Pallas kernels, row_call(): pl.pallas_call(kernel, grid=(total // step_rows,), in_specs=[row_spec(ste...  63.5 us
    ppermute x30, waiting for transfers between devices, swap(): lax.ppermute(piece, axis_name, [(place, place ^ 1 << bit) for place in ra...  58 us
    pallas_call x5, Pallas kernels, attend_backward(): pl.pallas_call(lambda *refs: attend_backward_kernel(step, *refs), out_sha...  48.5 us
    pallas_call x2, Pallas kernels, attend_forward(): pl.pallas_call(lambda *refs: attend_forward_kernel(causal, step, *refs),...  36.8 us
    ppermute x30, starting transfers between devices, swap(): lax.ppermute(piece, axis_name, [(place, place ^ 1 << bit) for place in ra...  34.2 us
    pallas_call x3, Pallas kernels, weight_parts(): pl.pallas_call(lambda *refs: weight_kernel(jobs, parcels, len(arrays), *r...  31.5 us
    convert_element_type x18, other arithmetic, step(): both = lambda which: (pick(kept, which).astype(high) + pick(received, whi...  27.8 us
    all_to_all x5, starting transfers between devices, exchange(): lax.all_to_all(piece, 'narrow', split_axis=0, concat_axis=0, tiled=True)  19.4 us
  transfers between devices with their start and end apart: 35, of which 11 were waited for; matrix products, arithmetic and copies ran while one was open for 11% of the time, Pallas kernels for 39%

profile of v2, /device:TPU:0, one launch (start us, length us, event | category | flops | bytes accessed | tf_op | source)
XLA Modules:
  0.0 385.7 jit_solution(9680455972541859984)
XLA Ops:
  0.7 16.5 %all_to_all.30 = bf16[4,128,768]{2,1,0:T(8,128)(2,1)} all-to-all(bf16[4,128,768]{2,1,0:T(8,128)(2,1)} %param.18), channel_id=1, replica_groups=mesh['items'=8,'narrow'=4] {'narrow'}, dimensions={0} | all-to-all | bytes 1572864 | tf_op jit(solution)/shard_map/all_to_all | solution.py:587
  17.2 3.8 all-to-all-start.1
  23.4 5.2 %enter_self.1 = (bf16[512,768]{1,0:T(8,128)(2,1)}, bf16[512,768]{1,0:T(8,128)(2,1)}, bf16[512,768]{1,0:T(8,128)(2,1)}, bf16[512,768]{1,0:T(8,128)(2,1)}) custom-call(bf16[512,768]{1,0:T(8,128)(2,1)} %bitcast.151, f32[1,768]{1,0:T(1,128)} %reshape.449.gain_ref, bf16[768,768]{1,0:T(8,128)(2,1)} %wq_ref.7, bf16[768,768]{1,0:T(8,128)(2,1)} %wk_ref.7, ...), custom_call_target="tpu_custom_call" | custom-call | flops 3625451520 | bytes 4328448 | tf_op jit(solution)/shard_map/enter_self/pallas_call | solution.py:75
  28.6 8.7 %self_forward.1 = (bf16[6,512,1024]{2,1,0:T(8,128)(2,1)}, bf16[512,768]{1,0:T(8,128)(2,1)}, f32[6,1,1024]{2,1,0:T(1,128)}) custom-call(s32[1]{0:T(128)} %dynamic_slice.247.refs_0_, bf16[512,768]{1,0:T(8,128)(2,1)} %get-tuple-element.118.refs_1_.refs_2_, bf16[512,768]{1,0:T(8,128)(2,1)} %get-tuple-element.119.refs_2_.refs_3_, ...), custom_call_target="tpu_custom_call" | custom-call | flops 3221225472 | bytes 2359296 | tf_op jit(solution)/shard_map/self_forward/pallas_call | solution.py:276
  37.3 5.0 %enter_cross.1 = (f32[512,768]{1,0:T(8,128)}, bf16[512,768]{1,0:T(8,128)(2,1)}, bf16[512,768]{1,0:T(8,128)(2,1)}) custom-call(bf16[512,768]{1,0:T(8,128)(2,1)} %get-tuple-element.121.attended_ref.refs_6_.refs_5_, bf16[512,768]{1,0:T(8,128)(2,1)} %bitcast.152, f32[1,768]{1,0:T(1,128)} %reshape.450.gain_ref, bf16[768,768]{1,0:T(8,128)(2,1)} %out_ref.5, ...), custom_call_target="tpu_custom_call" | custom-call | flops 2417491968 | bytes 3935232 | tf_op jit(solution)/shard_map/enter_cross/pallas_call | solution.py:75
  42.3 15.6 %all-to-all-done.1 = bf16[4,512,768]{2,1,0:T(8,128)(2,1)S(1)} async-done(((bf16[4,512,768]{2,1,0:T(8,128)(2,1)}), bf16[4,512,768]{2,1,0:T(8,128)(2,1)S(1)}, u32[]{:S(2)}, u32[]{:S(2)}) %all-to-all-start.1) | async-done | bytes 3145760 | tf_op jit(solution)/shard_map/all_to_all | solution.py:587
  57.9 4.7 %all-to-all-start.2 = ((bf16[4,128,768]{2,1,0:T(8,128)(2,1)}), bf16[4,128,768]{2,1,0:T(8,128)(2,1)}, u32[]{:S(2)}, u32[]{:S(2)}) async-start(bf16[4,128,768]{2,1,0:T(8,128)(2,1)} %param.21), calls=%async_computation.2 | async-start | bytes 1572864 | tf_op jit(solution)/shard_map/all_to_all | solution.py:587
  62.6 8.4 %enter_memory.1 = (bf16[2048,768]{1,0:T(8,128)(2,1)}, bf16[2048,768]{1,0:T(8,128)(2,1)}) custom-call(bf16[2048,768]{1,0:T(8,128)(2,1)} %bitcast.137, bf16[768,768]{1,0:T(8,128)(2,1)} %wk_ref.6, bf16[768,768]{1,0:T(8,128)(2,1)} %wv_ref.6), custom_call_target="tpu_custom_call" | custom-call | flops 9663676416 | bytes 5505024 | tf_op jit(solution)/shard_map/enter_memory/pallas_call | solution.py:75
  71.0 28.1 %cross_forward.1 = (bf16[6,2048,1024]{2,1,0:T(8,128)(2,1)}, bf16[512,768]{1,0:T(8,128)(2,1)}, f32[6,1,1024]{2,1,0:T(1,128)}) custom-call(s32[1]{0:T(128)} %dynamic_slice.247.refs_0_, bf16[512,768]{1,0:T(8,128)(2,1)} %get-tuple-element.122.refs_1_.refs_2_, bf16[2048,768]{1,0:T(8,128)(2,1)} %get-tuple-element.123.refs_2_.refs_3_, ...), custom_call_target="tpu_custom_call" | custom-call | flops 12884901888 | bytes 7077888 | tf_op jit(solution)/shard_map/cross_forward/pallas_call | solution.py:276
  99.1 22.8 %feed_both.1 = (bf16[512,768]{1,0:T(8,128)(2,1)}, bf16[512,2048]{1,0:T(8,128)(2,1)}, bf16[512,2048]{1,0:T(8,128)(2,1)}, bf16[512,2048]{1,0:T(8,128)(2,1)}, bf16[...) custom-call(bf16[512,768]{1,0:T(8,128)(2,1)} %get-tuple-element.125., ...), custom_call_target="tpu_custom_call" | custom-call | flops 10873208832 | bytes 13765632 | tf_op jit(solution)/shard_map/feed_both/pallas_call | solution.py:75
  122.0 12.7 %feed_weights.1 = (bf16[8,1152,128]{2,1,0:T(8,128)(2,1)}, bf16[8,1152,128]{2,1,0:T(8,128)(2,1)}, bf16[8,1440,128]{2,1,0:T(8,128)(2,1)}, bf16[8,1440,128]{2,1,0:T(8,128)(2,1)}) custom-call(s32[1]{0:T(128)} %bitcast.4.refs_0_, bf16[512,768]{1,0:T(8,128)(2,1)} %get-tuple-element.133.refs_1_, bf16[512,2048]{1,0:T(8,128)(2,1)} %get-tuple-element.134.refs_2_, ...), custom_call_target="tpu_custom_call" | custom-call | flops 10871635968 | bytes 9437184 | tf_op jit(solution)/shard_map/feed_weights/pallas_call | solution.py:474
  135.2 11.9 %cross_backward.3 = (bf16[512,768]{1,0:T(8,128)(2,1)}, bf16[2048,768]{1,0:T(8,128)(2,1)}, bf16[2048,768]{1,0:T(8,128)(2,1)}) custom-call(bf16[6,2048,1024]{2,1,0:T(8,128)(2,1)} %get-tuple-element.130.refs_0_, f32[6,1,1024]{2,1,0:T(1,128)} %get-tuple-element.131.refs_1_, bf16[512,768]{1,0:T(8,128)(2,1)} %get-tuple-element.122.refs_1_.refs_2_, ...), custom_call_target="tpu_custom_call" | custom-call | flops 6442450944 | bytes 8388608 | tf_op jit(solution)/shard_map/cross_backward/pallas_call | solution.py:341
  147.2 1.6 copy-done.3
  148.8 4.7 %fusion.1 = (bf16[4,1440,128]{2,1,0:T(8,128)(2,1)}, bf16[4,1440,128]{2,1,0:T(8,128)(2,1)S(1)}) fusion(bf16[2,4,1440,128]{3,2,1,0:T(8,128)(2,1)} %bitcast.140, s32[]{:T(128)S(6)} %select_n.139, bf16[2,4,1440,128]{3,2,1,0:T(8,128)(2,1)} %bitcast.139, s32[]{:T(128)S(6)} %select_n.138), kind=kLoop, calls=%fused_computation.5 | loop fusion | flops 5898240 | bytes 8847368 | tf_op jit(solution)/shard_map/convert_element_type | solution.py:514
  153.5 2.4 collective-permute-start.26
  156.0 3.3 fusion.3
  159.2 1.5 collective-permute-start.1
  160.8 12.1 %cross_backward.4 = (bf16[512,768]{1,0:T(8,128)(2,1)}, bf16[2048,768]{1,0:T(8,128)(2,1)}, bf16[2048,768]{1,0:T(8,128)(2,1)}) custom-call(bf16[6,2048,1024]{2,1,0:T(8,128)(2,1)} %get-tuple-element.130.refs_0_, f32[6,1,1024]{2,1,0:T(1,128)} %get-tuple-element.131.refs_1_, ...), custom_call_target="tpu_custom_call", output_to_operand_aliasing={{0}: (7, {}), {1}: (8, {}), {2}: (9, {})} | custom-call | flops 6442450944 | bytes 8388608 | tf_op jit(solution)/shard_map/cross_backward/pallas_call | solution.py:341
  172.9 14.7 %collective-permute-done.1 = bf16[4,1152,128]{2,1,0:T(8,128)(2,1)} collective-permute-done((bf16[4,1152,128]{2,1,0:T(8,128)(2,1)}, bf16[4,1152,128]{2,1,0:T(8,128)(2,1)}, u32[]{:S(2)}, u32[]{:S(2)}) %collective-permute-start.1) | collective-permute-done | bytes 1179680 | tf_op jit(solution)/shard_map/ppermute | solution.py:371
  187.6 2.4 fusion.7
  190.3 11.9 %cross_backward.5 = (bf16[512,768]{1,0:T(8,128)(2,1)}, bf16[2048,768]{1,0:T(8,128)(2,1)}, bf16[2048,768]{1,0:T(8,128)(2,1)}) custom-call(bf16[6,2048,1024]{2,1,0:T(8,128)(2,1)} %get-tuple-element.130.refs_0_, f32[6,1,1024]{2,1,0:T(1,128)} %get-tuple-element.131.refs_1_, ...), custom_call_target="tpu_custom_call", output_to_operand_aliasing={{0}: (7, {}), {1}: (8, {}), {2}: (9, {})} | custom-call | flops 6442450944 | bytes 8388608 | tf_op jit(solution)/shard_map/cross_backward/pallas_call | solution.py:341
  202.2 2.6 collective-permute-done.2
  205.7 2.6 collective-permute-start.3
  208.3 6.2 %leave_cross.1 = (f32[512,768]{1,0:T(8,128)}, bf16[512,768]{1,0:T(8,128)(2,1)}, bf16[512,768]{1,0:T(8,128)(2,1)}, f32[1,768]{1,0:T(1,128)}) custom-call(bf16[512,768]{1,0:T(8,128)(2,1)} %get-tuple-element.156.grad_q_ref.refs_5_, f32[512,768]{1,0:T(8,128)} %get-tuple-element.126.hidden_ref, f32[512,768]{1,0:T(8,128)} %get-tuple-element.157.grad_in_ref, ...), custom_call_target="tpu_custom_call" | custom-call | flops 2417491968 | bytes 6294528 | tf_op jit(solution)/shard_map/leave_cross/pallas_call | solution.py:75
  214.5 1.7 fusion.5
  216.2 1.6 collective-permute-start.27
  217.8 9.4 %leave_memory.1 = bf16[2048,768]{1,0:T(8,128)(2,1)} custom-call(bf16[2048,768]{1,0:T(8,128)(2,1)} %get-tuple-element.165.grad_k_ref.refs_2_, bf16[2048,768]{1,0:T(8,128)(2,1)} %get-tuple-element.162.grad_v_ref.refs_3_, bf16[768,768]{1,0:T(8,128)(2,1)} %wk_ref.6, bf16[768,768]{1,0:T(8,128)(2,1)} %wv_ref.6), custom_call_target="tpu_custom_call" | custom-call | flops 4831838208 | bytes 8650752 | tf_op jit(solution)/shard_map/leave_memory/pallas_call | solution.py:75
  228.1 12.8 %cross_weights.1 = (bf16[8,576,128]{2,1,0:T(8,128)(2,1)}, bf16[8,576,128]{2,1,0:T(8,128)(2,1)}, bf16[8,576,128]{2,1,0:T(8,128)(2,1)}, bf16[8,576,128]{2,1,0:T(8,128)(2,1)}) custom-call(s32[1]{0:T(128)} %bitcast.4.refs_0_, bf16[2048,768]{1,0:T(8,128)(2,1)} %bitcast.138, bf16[2048,768]{1,0:T(8,128)(2,1)} %get-tuple-element.165.grad_k_ref.refs_2_, ...), custom_call_target="tpu_custom_call" | custom-call | flops 12079595520 | bytes 12582912 | tf_op jit(solution)/shard_map/cross_weights/pallas_call | solution.py:474
  242.0 3.7 all-to-all-start.3
  245.7 2.1 collective-permute-start.24
  247.8 6.2 %self_backward.2 = (bf16[512,768]{1,0:T(8,128)(2,1)}, bf16[512,768]{1,0:T(8,128)(2,1)}, bf16[512,768]{1,0:T(8,128)(2,1)}) custom-call(bf16[6,512,1024]{2,1,0:T(8,128)(2,1)} %get-tuple-element.128.refs_0_, f32[6,1,1024]{2,1,0:T(1,128)} %get-tuple-element.129.refs_1_, bf16[512,768]{1,0:T(8,128)(2,1)} %get-tuple-element.118.refs_1_.refs_2_, ...), custom_call_target="tpu_custom_call" | custom-call | flops 2415919104 | bytes 3145728 | tf_op jit(solution)/shard_map/self_backward/pallas_call | solution.py:341
  254.0 6.8 %collective-permute-done.28 = bf16[1,1440,128]{2,1,0:T(8,128)(2,1)S(1)} collective-permute-done((bf16[1,1440,128]{2,1,0:T(8,128)(2,1)S(1)}, bf16[1,1440,128]{2,1,0:T(8,128)(2,1)S(1)}, u32[]{:S(2)}, u32[]{:S(2)}) %collective-permute-start.28) | collective-permute-done | bytes 368672 | tf_op jit(solution)/shard_map/ppermute | solution.py:371
  260.9 1.9 fusion.9
  262.8 6.3 %self_backward.3 = (bf16[512,768]{1,0:T(8,128)(2,1)}, bf16[512,768]{1,0:T(8,128)(2,1)}, bf16[512,768]{1,0:T(8,128)(2,1)}) custom-call(bf16[6,512,1024]{2,1,0:T(8,128)(2,1)} %get-tuple-element.128.refs_0_, f32[6,1,1024]{2,1,0:T(1,128)} %get-tuple-element.129.refs_1_, ...), custom_call_target="tpu_custom_call", output_to_operand_aliasing={{0}: (7, {}), {1}: (8, {}), {2}: (9, {})} | custom-call | flops 2415919104 | bytes 3145728 | tf_op jit(solution)/shard_map/self_backward/pallas_call | solution.py:341
  269.0 6.4 %leave_self.1 = (bf16[512,768]{1,0:T(8,128)(2,1)}, f32[1,768]{1,0:T(1,128)}) custom-call(bf16[512,768]{1,0:T(8,128)(2,1)} %get-tuple-element.176.grad_q_ref.refs_2_, bf16[512,768]{1,0:T(8,128)(2,1)} %get-tuple-element.177.grad_k_ref.refs_3_, bf16[512,768]{1,0:T(8,128)(2,1)} %get-tuple-element.178.grad_v_ref.refs_4_, bf16[512,768]{1,0:T(8,128)(2,1)} %bitcast.153, ...), custom_call_target="tpu_custom_call" | custom-call | flops 3625451520 | bytes 8260608 | tf_op jit(solution)/shard_map/leave_self/pallas_call | solution.py:75
  276.8 6.0 %self_weights.1 = (bf16[8,464,128]{2,1,0:T(8,128)(2,1)}, bf16[8,464,128]{2,1,0:T(8,128)(2,1)}, bf16[8,432,128]{2,1,0:T(8,128)(2,1)}, bf16[8,432,128]{2,1,0:T(8,128)(2,1)}) custom-call(s32[1]{0:T(128)} %bitcast.4.refs_0_, bf16[512,768]{1,0:T(8,128)(2,1)} %get-tuple-element.181.refs_1_, bf16[512,768]{1,0:T(8,128)(2,1)} %get-tuple-element.176.grad_q_ref.refs_2_, ...), custom_call_target="tpu_custom_call" | custom-call | flops 3623878656 | bytes 3153920 | tf_op jit(solution)/shard_map/self_weights/pallas_call | solution.py:474
  282.8 1.9 fusion.11
  285.8 14.7 %collective-permute-done.20 = bf16[4,576,128]{2,1,0:T(8,128)(2,1)S(1)} collective-permute-done((bf16[4,576,128]{2,1,0:T(8,128)(2,1)S(1)}, bf16[4,576,128]{2,1,0:T(8,128)(2,1)S(1)}, u32[]{:S(2)}, u32[]{:S(2)}) %collective-permute-start.20) | collective-permute-done | bytes 589856 | tf_op jit(solution)/shard_map/ppermute | solution.py:371
  304.9 1.3 collective-permute-start.29
  306.2 3.5 all-to-all-start.4
  309.7 2.7 add_convert_fusion.15
  312.4 1.7 collective-permute-start.11
  315.9 2.9 collective-permute-start.17
  318.8 2.3 add_convert_fusion.13
  321.1 6.8 %collective-permute-done.22 = bf16[1,576,128]{2,1,0:T(8,128)(2,1)S(1)} collective-permute-done((bf16[1,576,128]{2,1,0:T(8,128)(2,1)S(1)}, bf16[1,576,128]{2,1,0:T(8,128)(2,1)S(1)}, u32[]{:S(2)}, u32[]{:S(2)}) %collective-permute-start.22) | collective-permute-done | bytes 147488 | tf_op jit(solution)/shard_map/ppermute | solution.py:371
  327.9 1.5 collective-permute-start.6
  329.5 1.6 add_convert_fusion.30
  332.0 3.7 all-to-all-start.5
  340.2 2.0 collective-permute-start.18
  343.4 1.6 collective-permute-start.7
  344.9 1.9 collective-permute-done.12
  346.8 3.4 collective-permute-start.13
  350.9 3.4 collective-permute-done.13
  354.3 2.5 collective-permute-start.23
  357.8 5.7 %collective-permute-done.8 = bf16[1,464,128]{2,1,0:T(8,128)(2,1)S(1)} collective-permute-done((bf16[1,464,128]{2,1,0:T(8,128)(2,1)S(1)}, bf16[1,464,128]{2,1,0:T(8,128)(2,1)S(1)}, u32[]{:S(2)}, u32[]{:S(2)}) %collective-permute-start.8) | collective-permute-done | bytes 118816 | tf_op jit(solution)/shard_map/ppermute | solution.py:371
  365.4 1.5 collective-permute-start.14
  367.0 2.1 feed_weights_end.1
  369.1 1.7 copy.44
  370.8 2.4 convert_element_type.652
  373.3 3.2 convert_element_type.653
  377.9 1.9 cross_weights_end.1
  380.2 1.8 self_weights_end.1
  382.0 1.4 slice_bitcast_fusion.6
  383.4 2.1 copy.55
  (116 shorter events, 26.5 us)
Async XLA Ops:
  17.2 3.9 %copy-start.12 = (f32[768]{0:T(1024)S(1)}, f32[768]{0:T(1024)}, u32[]{:S(2)}) copy-start(f32[768]{0:T(1024)} %param.22) | copy-start | bytes 9220
  17.2 4.5 %copy-start.13 = (f32[768]{0:T(1024)S(1)}, f32[768]{0:T(1024)}, u32[]{:S(2)}) copy-start(f32[768]{0:T(1024)} %param.27) | copy-start | bytes 9220
  17.2 5.0 %copy-start.14 = (f32[768]{0:T(1024)S(1)}, f32[768]{0:T(1024)}, u32[]{:S(2)}) copy-start(f32[768]{0:T(1024)} %param.32) | copy-start | bytes 9220
  17.2 5.6 %copy-start.17 = (s32[4]{0:T(128)S(1)}, s32[4]{0:T(128)}, u32[]{:S(2)}) copy-start(s32[4]{0:T(128)} %param.20) | copy-start | bytes 52
  17.2 40.8 %all-to-all-start.1 = ((bf16[4,512,768]{2,1,0:T(8,128)(2,1)}), bf16[4,512,768]{2,1,0:T(8,128)(2,1)S(1)}, u32[]{:S(2)}, u32[]{:S(2)}) async-start(bf16[4,512,768]{2,1,0:T(8,128)(2,1)} %param.19), calls=%async_computation.1 | async-start | bytes 6291456 | tf_op jit(solution)/shard_map/all_to_all | solution.py:587
  57.9 4.7 %copy-start = (bf16[4,512,768]{2,1,0:T(8,128)(2,1)}, bf16[4,512,768]{2,1,0:T(8,128)(2,1)S(1)}, u32[]{:S(2)}) copy-start(bf16[4,512,768]{2,1,0:T(8,128)(2,1)S(1)} %all-to-all-done.1) | copy-start | bytes 9437188
  57.9 41.2 %all-to-all-start.2 = ((bf16[4,128,768]{2,1,0:T(8,128)(2,1)}), bf16[4,128,768]{2,1,0:T(8,128)(2,1)}, u32[]{:S(2)}, u32[]{:S(2)}) async-start(bf16[4,128,768]{2,1,0:T(8,128)(2,1)} %param.21), calls=%async_computation.2 | async-start | bytes 1572864 | tf_op jit(solution)/shard_map/all_to_all | solution.py:587
  134.7 12.5 %collective-permute-start.25 = (bf16[8,1440,128]{2,1,0:T(8,128)(2,1)}, bf16[8,1440,128]{2,1,0:T(8,128)(2,1)S(1)}, u32[]{:S(2)}, u32[]{:S(2)}) collective-permute-start(bf16[8,1440,128]{2,1,0:T(8,128)(2,1)} %get-tuple-element.206), channel_id=1, source_target_pairs={{0,1},{1,0},{2,3},{3,2},{4,5},{5,4},{6,7},{7,6},{8,9},{9,8},{10,11... | collective-permute-start | bytes 8847368 | tf_op jit(solution)/shard_map/ppermute | solution.py:371
  135.2 12.0 %collective-permute-start = (bf16[8,1152,128]{2,1,0:T(8,128)(2,1)}, bf16[8,1152,128]{2,1,0:T(8,128)(2,1)}, u32[]{:S(2)}, u32[]{:S(2)}) collective-permute-start(bf16[8,1152,128]{2,1,0:T(8,128)(2,1)} %get-tuple-element.139), channel_id=1, source_target_pairs={{0,1},{1,0},{2,3},{3,2},{4,5},{5,4},{6,7},{7,6},{8,9},{9,8},{10,11... | collective-permute-start | bytes 7077896 | tf_op jit(solution)/shard_map/ppermute | solution.py:371
  147.2 1.6 copy-start.3
  148.8 7.1 %copy-start.4 = (bf16[8,1152,128]{2,1,0:T(8,128)(2,1)S(1)}, bf16[8,1152,128]{2,1,0:T(8,128)(2,1)}, u32[]{:S(2)}) copy-start(bf16[8,1152,128]{2,1,0:T(8,128)(2,1)} %get-tuple-element.142) | copy-start | bytes 7077892
  153.5 36.7 %collective-permute-start.26 = (bf16[4,1440,128]{2,1,0:T(8,128)(2,1)}, bf16[4,1440,128]{2,1,0:T(8,128)(2,1)}, u32[]{:S(2)}, u32[]{:S(2)}) collective-permute-start(bf16[4,1440,128]{2,1,0:T(8,128)(2,1)} %get-tuple-element.236), channel_id=1, source_target_pairs={{0,8},{4,12},{8,0},{12,4},{16,24},{20,28},{24,16},{28,20},{1,9},{5... | collective-permute-start | bytes 4423688 | tf_op jit(solution)/shard_map/ppermute | solution.py:371
  159.2 28.4 %collective-permute-start.1 = (bf16[4,1152,128]{2,1,0:T(8,128)(2,1)}, bf16[4,1152,128]{2,1,0:T(8,128)(2,1)}, u32[]{:S(2)}, u32[]{:S(2)}) collective-permute-start(bf16[4,1152,128]{2,1,0:T(8,128)(2,1)} %get-tuple-element.238), channel_id=1, source_target_pairs={{0,4},{4,0},{8,12},{12,8},{16,20},{20,16},{24,28},{28,24},{1,5},{5... | collective-permute-start | bytes 3538952 | tf_op jit(solution)/shard_map/ppermute | solution.py:371
  190.0 14.8 %collective-permute-start.2 = (bf16[2,1152,128]{2,1,0:T(8,128)(2,1)}, bf16[2,1152,128]{2,1,0:T(8,128)(2,1)S(1)}, u32[]{:S(2)}, u32[]{:S(2)}) collective-permute-start(bf16[2,1152,128]{2,1,0:T(8,128)(2,1)} %get-tuple-element.246), channel_id=1, source_target_pairs={{0,8},{4,12},{8,0},{12,4},{16,24},{20,28},{24,16},{28,20},{1,9},{5... | collective-permute-start | bytes 1769480 | tf_op jit(solution)/shard_map/ppermute | solution.py:371
  205.7 21.5 %collective-permute-start.3 = (bf16[1,1152,128]{2,1,0:T(8,128)(2,1)}, bf16[1,1152,128]{2,1,0:T(8,128)(2,1)S(1)}, u32[]{:S(2)}, u32[]{:S(2)}) collective-permute-start(bf16[1,1152,128]{2,1,0:T(8,128)(2,1)} %get-tuple-element.258), channel_id=1, source_target_pairs={{0,16},{4,20},{8,24},{12,28},{16,0},{20,4},{24,8},{28,12},{1,17},{... | collective-permute-start | bytes 884744 | tf_op jit(solution)/shard_map/ppermute | solution.py:371
  216.2 25.2 %collective-permute-start.27 = (bf16[2,1440,128]{2,1,0:T(8,128)(2,1)S(1)}, bf16[2,1440,128]{2,1,0:T(8,128)(2,1)S(1)}, u32[]{:S(2)}, u32[]{:S(2)}) collective-permute-start(bf16[2,1440,128]{2,1,0:T(8,128)(2,1)S(1)} %get-tuple-element.240), channel_id=1, source_target_pairs={{0,4},{4,0},{8,12},{12,8},{16,20},{20,16},{24,28},{28,24},{1,5},{5... | collective-permute-start | bytes 2211848 | tf_op jit(solution)/shard_map/ppermute | solution.py:371
  240.9 20.0 %collective-permute-start.19 = (bf16[8,576,128]{2,1,0:T(8,128)(2,1)}, bf16[8,576,128]{2,1,0:T(8,128)(2,1)}, u32[]{:S(2)}, u32[]{:S(2)}) collective-permute-start(bf16[8,576,128]{2,1,0:T(8,128)(2,1)} %get-tuple-element.196), channel_id=1, source_target_pairs={{0,1},{1,0},{2,3},{3,2},{4,5},{5,4},{6,7},{7,6},{8,9},{9,8},{10,11... | collective-permute-start | bytes 3538952 | tf_op jit(solution)/shard_map/ppermute | solution.py:371
  240.9 20.0 %collective-permute-start.4 = (bf16[8,576,128]{2,1,0:T(8,128)(2,1)}, bf16[8,576,128]{2,1,0:T(8,128)(2,1)}, u32[]{:S(2)}, u32[]{:S(2)}) collective-permute-start(bf16[8,576,128]{2,1,0:T(8,128)(2,1)} %get-tuple-element.168), channel_id=1, source_target_pairs={{0,1},{1,0},{2,3},{3,2},{4,5},{5,4},{6,7},{7,6},{8,9},{9,8},{10,11... | collective-permute-start | bytes 3538952 | tf_op jit(solution)/shard_map/ppermute | solution.py:371
  241.4 4.3 %copy-start.15 = (f32[1,768]{1,0:T(1,128)S(1)}, f32[1,768]{1,0:T(1,128)}, u32[]{:S(2)}) copy-start(f32[1,768]{1,0:T(1,128)} %get-tuple-element.184) | copy-start | bytes 9220
  241.4 4.3 %copy-start.16 = (f32[1,768]{1,0:T(1,128)S(1)}, f32[1,768]{1,0:T(1,128)}, u32[]{:S(2)}) copy-start(f32[1,768]{1,0:T(1,128)} %get-tuple-element.183) | copy-start | bytes 9220
  241.6 19.3 %collective-permute-start.28 = (bf16[1,1440,128]{2,1,0:T(8,128)(2,1)S(1)}, bf16[1,1440,128]{2,1,0:T(8,128)(2,1)S(1)}, u32[]{:S(2)}, u32[]{:S(2)}) collective-permute-start(bf16[1,1440,128]{2,1,0:T(8,128)(2,1)S(1)} %get-tuple-element.252), channel_id=1, source_target_pairs={{0,16},{4,20},{8,24},{12,28},{16,0},{20,4},{24,8},{28,12},{1,17},{... | collective-permute-start | bytes 1105928 | tf_op jit(solution)/shard_map/ppermute | solution.py:371
  242.0 64.2 %all-to-all-start.3 = ((bf16[4,128,768]{2,1,0:T(8,128)(2,1)}), bf16[4,128,768]{2,1,0:T(8,128)(2,1)S(1)}, u32[]{:S(2)}, u32[]{:S(2)}) async-start(bf16[4,128,768]{2,1,0:T(8,128)(2,1)} %bitcast.3), calls=%async_computation.3 | async-start | bytes 1572864 | tf_op jit(solution)/shard_map/all_to_all | solution.py:587
  245.7 119.7 %collective-permute-start.24 = (bf16[640,128]{1,0:T(8,128)(2,1)}, bf16[640,128]{1,0:T(8,128)(2,1)}, u32[]{:S(2)}, u32[]{:S(2)}) collective-permute-start(bf16[640,128]{1,0:T(8,128)(2,1)} %get-tuple-element.289), channel_id=1, source_target_pairs={{0,2},{1,3},{2,0},{3,1},{4,6},{5,7},{6,4},{7,5},{8,10},{9,11},{10,... | collective-permute-start | bytes 491528 | tf_op jit(solution)/shard_map/ppermute | solution.py:371
  282.8 21.2 %collective-permute-start.10 = (bf16[8,432,128]{2,1,0:T(8,128)(2,1)}, bf16[8,432,128]{2,1,0:T(8,128)(2,1)S(1)}, u32[]{:S(2)}, u32[]{:S(2)}) collective-permute-start(bf16[8,432,128]{2,1,0:T(8,128)(2,1)} %get-tuple-element.188), channel_id=1, source_target_pairs={{0,1},{1,0},{2,3},{3,2},{4,5},{5,4},{6,7},{7,6},{8,9},{9,8},{10,11... | collective-permute-start | bytes 2654216 | tf_op jit(solution)/shard_map/ppermute | solution.py:371
  284.7 15.8 %collective-permute-start.20 = (bf16[4,576,128]{2,1,0:T(8,128)(2,1)S(1)}, bf16[4,576,128]{2,1,0:T(8,128)(2,1)S(1)}, u32[]{:S(2)}, u32[]{:S(2)}) collective-permute-start(bf16[4,576,128]{2,1,0:T(8,128)(2,1)S(1)} %get-tuple-element.242), channel_id=1, source_target_pairs={{0,8},{4,12},{8,0},{12,4},{16,24},{20,28},{24,16},{28,20},{1,9},{5... | collective-permute-start | bytes 1769480 | tf_op jit(solution)/shard_map/ppermute | solution.py:371
  284.8 17.1 %collective-permute-start.15 = (bf16[4,576,128]{2,1,0:T(8,128)(2,1)S(1)}, bf16[4,576,128]{2,1,0:T(8,128)(2,1)S(1)}, u32[]{:S(2)}, u32[]{:S(2)}) collective-permute-start(bf16[4,576,128]{2,1,0:T(8,128)(2,1)S(1)} %get-tuple-element.244), channel_id=1, source_target_pairs={{0,4},{4,0},{8,12},{12,8},{16,20},{20,16},{24,28},{28,24},{1,5},{5... | collective-permute-start | bytes 1769480 | tf_op jit(solution)/shard_map/ppermute | solution.py:371
  285.5 30.4 %collective-permute-start.5 = (bf16[8,464,128]{2,1,0:T(8,128)(2,1)}, bf16[8,464,128]{2,1,0:T(8,128)(2,1)}, u32[]{:S(2)}, u32[]{:S(2)}) collective-permute-start(bf16[8,464,128]{2,1,0:T(8,128)(2,1)} %get-tuple-element.186), channel_id=1, source_target_pairs={{0,1},{1,0},{2,3},{3,2},{4,5},{5,4},{6,7},{7,6},{8,9},{9,8},{10,11... | collective-permute-start | bytes 2850824 | tf_op jit(solution)/shard_map/ppermute | solution.py:371
  301.4 11.0 %collective-permute-start.21 = (bf16[2,576,128]{2,1,0:T(8,128)(2,1)}, bf16[2,576,128]{2,1,0:T(8,128)(2,1)}, u32[]{:S(2)}, u32[]{:S(2)}) collective-permute-start(bf16[2,576,128]{2,1,0:T(8,128)(2,1)} %get-tuple-element.255), channel_id=1, source_target_pairs={{0,4},{4,0},{8,12},{12,8},{16,20},{20,16},{24,28},{28,24},{1,5},{5... | collective-permute-start | bytes 884744 | tf_op jit(solution)/shard_map/ppermute | solution.py:371
  302.8 12.2 %collective-permute-start.16 = (bf16[2,576,128]{2,1,0:T(8,128)(2,1)}, bf16[2,576,128]{2,1,0:T(8,128)(2,1)S(1)}, u32[]{:S(2)}, u32[]{:S(2)}) collective-permute-start(bf16[2,576,128]{2,1,0:T(8,128)(2,1)} %get-tuple-element.257), channel_id=1, source_target_pairs={{0,8},{4,12},{8,0},{12,4},{16,24},{20,28},{24,16},{28,20},{1,9},{5... | collective-permute-start | bytes 884744 | tf_op jit(solution)/shard_map/ppermute | solution.py:371
  304.0 0.9 copy-start.8
  304.9 62.1 %collective-permute-start.29 = (bf16[832,128]{1,0:T(8,128)(2,1)}, bf16[832,128]{1,0:T(8,128)(2,1)}, u32[]{:S(2)}, u32[]{:S(2)}) collective-permute-start(bf16[832,128]{1,0:T(8,128)(2,1)} %get-tuple-element.279), channel_id=1, source_target_pairs={{0,2},{1,3},{2,0},{3,1},{4,6},{5,7},{6,4},{7,5},{8,10},{9,11},{10,... | collective-permute-start | bytes 638984 | tf_op jit(solution)/shard_map/ppermute | solution.py:371
  306.2 6.2 %copy-start.1 = (bf16[4,128,768]{2,1,0:T(8,128)(2,1)}, bf16[4,128,768]{2,1,0:T(8,128)(2,1)S(1)}, u32[]{:S(2)}) copy-start(bf16[4,128,768]{2,1,0:T(8,128)(2,1)S(1)} %all-to-all-done.3) | copy-start | bytes 2359300
  306.2 24.9 %all-to-all-start.4 = ((bf16[4,128,768]{2,1,0:T(8,128)(2,1)}), bf16[4,128,768]{2,1,0:T(8,128)(2,1)S(1)}, u32[]{:S(2)}, u32[]{:S(2)}) async-start(bf16[4,128,768]{2,1,0:T(8,128)(2,1)} %bitcast.18), calls=%async_computation.4 | async-start | bytes 1572864 | tf_op jit(solution)/shard_map/all_to_all | solution.py:587
  309.7 9.1 %copy-start.7 = (bf16[8,464,128]{2,1,0:T(8,128)(2,1)S(1)}, bf16[8,464,128]{2,1,0:T(8,128)(2,1)}, u32[]{:S(2)}) copy-start(bf16[8,464,128]{2,1,0:T(8,128)(2,1)} %get-tuple-element.185) | copy-start | bytes 2850820
  312.4 25.4 %collective-permute-start.11 = (bf16[4,432,128]{2,1,0:T(8,128)(2,1)}, bf16[4,432,128]{2,1,0:T(8,128)(2,1)}, u32[]{:S(2)}, u32[]{:S(2)}) collective-permute-start(bf16[4,432,128]{2,1,0:T(8,128)(2,1)} %get-tuple-element.251), channel_id=1, source_target_pairs={{0,8},{4,12},{8,0},{12,4},{16,24},{20,28},{24,16},{28,20},{1,9},{5... | collective-permute-start | bytes 1327112 | tf_op jit(solution)/shard_map/ppermute | solution.py:371
  315.1 6.1 %copy-start.9 = (bf16[2,576,128]{2,1,0:T(8,128)(2,1)}, bf16[2,576,128]{2,1,0:T(8,128)(2,1)S(1)}, u32[]{:S(2)}) copy-start(bf16[2,576,128]{2,1,0:T(8,128)(2,1)S(1)} %collective-permute-done.16) | copy-start | bytes 884740
  315.1 12.9 %collective-permute-start.22 = (bf16[1,576,128]{2,1,0:T(8,128)(2,1)S(1)}, bf16[1,576,128]{2,1,0:T(8,128)(2,1)S(1)}, u32[]{:S(2)}, u32[]{:S(2)}) collective-permute-start(bf16[1,576,128]{2,1,0:T(8,128)(2,1)S(1)} %fusion.16), channel_id=1, source_target_pairs={{0,16},{4,20},{8,24},{12,28},{16,0},{20,4},{24,8},{28,12},{1,17},{... | collective-permute-start | bytes 442376 | tf_op jit(solution)/shard_map/ppermute | solution.py:371
  315.9 19.9 %collective-permute-start.17 = (bf16[1,576,128]{2,1,0:T(8,128)(2,1)}, bf16[1,576,128]{2,1,0:T(8,128)(2,1)}, u32[]{:S(2)}, u32[]{:S(2)}) collective-permute-start(bf16[1,576,128]{2,1,0:T(8,128)(2,1)} %fusion.18), channel_id=1, source_target_pairs={{0,16},{4,20},{8,24},{12,28},{16,0},{20,4},{24,8},{28,12},{1,17},{... | collective-permute-start | bytes 442376 | tf_op jit(solution)/shard_map/ppermute | solution.py:371
  327.9 14.2 %collective-permute-start.6 = (bf16[4,464,128]{2,1,0:T(8,128)(2,1)}, bf16[4,464,128]{2,1,0:T(8,128)(2,1)}, u32[]{:S(2)}, u32[]{:S(2)}) collective-permute-start(bf16[4,464,128]{2,1,0:T(8,128)(2,1)} %get-tuple-element.249), channel_id=1, source_target_pairs={{0,4},{4,0},{8,12},{12,8},{16,20},{20,16},{24,28},{28,24},{1,5},{5... | collective-permute-start | bytes 1425416 | tf_op jit(solution)/shard_map/ppermute | solution.py:371
  331.1 0.9 copy-start.2
  332.0 41.3 %all-to-all-start.5 = ((bf16[4,512,768]{2,1,0:T(8,128)(2,1)}), bf16[4,512,768]{2,1,0:T(8,128)(2,1)S(1)}, u32[]{:S(2)}, u32[]{:S(2)}) async-start(bf16[4,512,768]{2,1,0:T(8,128)(2,1)} %bitcast.136), calls=%async_computation.5 | async-start | bytes 6291456 | tf_op jit(solution)/shard_map/all_to_all | solution.py:587
  335.7 2.1 copy-start.6
  335.7 6.5 %copy-start.5 = (bf16[1,4,464,128]{3,2,1,0:T(8,128)(2,1)S(1)}, bf16[1,4,464,128]{3,2,1,0:T(8,128)(2,1)}, u32[]{:S(2)}) copy-start(bf16[1,4,464,128]{3,2,1,0:T(8,128)(2,1)} %get-tuple-element.248) | copy-start | bytes 1425412
  338.9 7.8 %collective-permute-start.12 = (bf16[2,432,128]{2,1,0:T(8,128)(2,1)S(1)}, bf16[2,432,128]{2,1,0:T(8,128)(2,1)S(1)}, u32[]{:S(2)}, u32[]{:S(2)}) collective-permute-start(bf16[2,432,128]{2,1,0:T(8,128)(2,1)S(1)} %get-tuple-element.263), channel_id=1, source_target_pairs={{0,4},{4,0},{8,12},{12,8},{16,20},{20,16},{24,28},{28,24},{1,5},{5... | collective-permute-start | bytes 663560 | tf_op jit(solution)/shard_map/ppermute | solution.py:371
  340.2 36.3 %collective-permute-start.18 = (bf16[384,128]{1,0:T(8,128)(2,1)S(1)}, bf16[384,128]{1,0:T(8,128)(2,1)S(1)}, u32[]{:S(2)}, u32[]{:S(2)}) collective-permute-start(bf16[384,128]{1,0:T(8,128)(2,1)S(1)} %get-tuple-element.283), channel_id=1, source_target_pairs={{0,2},{1,3},{2,0},{3,1},{4,6},{5,7},{6,4},{7,5},{8,10},{9,11},{10,... | collective-permute-start | bytes 294920 | tf_op jit(solution)/shard_map/ppermute | solution.py:371
  343.4 13.5 %collective-permute-start.7 = (bf16[2,464,128]{2,1,0:T(8,128)(2,1)S(1)}, bf16[2,464,128]{2,1,0:T(8,128)(2,1)S(1)}, u32[]{:S(2)}, u32[]{:S(2)}) collective-permute-start(bf16[2,464,128]{2,1,0:T(8,128)(2,1)S(1)} %get-tuple-element.261), channel_id=1, source_target_pairs={{0,8},{4,12},{8,0},{12,4},{16,24},{20,28},{24,16},{28,20},{1,9},{5... | collective-permute-start | bytes 712712 | tf_op jit(solution)/shard_map/ppermute | solution.py:371
  346.8 7.5 %collective-permute-start.13 = (bf16[1,432,128]{2,1,0:T(8,128)(2,1)S(1)}, bf16[1,432,128]{2,1,0:T(8,128)(2,1)S(1)}, u32[]{:S(2)}, u32[]{:S(2)}) collective-permute-start(bf16[1,432,128]{2,1,0:T(8,128)(2,1)S(1)} %fusion.24), channel_id=1, source_target_pairs={{0,16},{4,20},{8,24},{12,28},{16,0},{20,4},{24,8},{28,12},{1,17},{... | collective-permute-start | bytes 331784 | tf_op jit(solution)/shard_map/ppermute | solution.py:371
  354.3 23.0 %collective-permute-start.23 = (bf16[384,128]{1,0:T(8,128)(2,1)S(1)}, bf16[384,128]{1,0:T(8,128)(2,1)S(1)}, u32[]{:S(2)}, u32[]{:S(2)}) collective-permute-start(bf16[384,128]{1,0:T(8,128)(2,1)S(1)} %get-tuple-element.281), channel_id=1, source_target_pairs={{0,2},{1,3},{2,0},{3,1},{4,6},{5,7},{6,4},{7,5},{8,10},{9,11},{10,... | collective-permute-start | bytes 294920 | tf_op jit(solution)/shard_map/ppermute | solution.py:371
  356.9 6.6 %collective-permute-start.8 = (bf16[1,464,128]{2,1,0:T(8,128)(2,1)S(1)}, bf16[1,464,128]{2,1,0:T(8,128)(2,1)S(1)}, u32[]{:S(2)}, u32[]{:S(2)}) collective-permute-start(bf16[1,464,128]{2,1,0:T(8,128)(2,1)S(1)} %fusion.21), channel_id=1, source_target_pairs={{0,16},{4,20},{8,24},{12,28},{16,0},{20,4},{24,8},{28,12},{1,17},{... | collective-permute-start | bytes 356360 | tf_op jit(solution)/shard_map/ppermute | solution.py:371
  364.3 16.0 %collective-permute-start.9 = (bf16[320,128]{1,0:T(8,128)(2,1)}, bf16[320,128]{1,0:T(8,128)(2,1)}, u32[]{:S(2)}, u32[]{:S(2)}) collective-permute-start(bf16[320,128]{1,0:T(8,128)(2,1)} %get-tuple-element.285), channel_id=1, source_target_pairs={{0,2},{1,3},{2,0},{3,1},{4,6},{5,7},{6,4},{7,5},{8,10},{9,11},{10,... | collective-permute-start | bytes 245768 | tf_op jit(solution)/shard_map/ppermute | solution.py:371
  365.4 14.8 %collective-permute-start.14 = (bf16[288,128]{1,0:T(8,128)(2,1)}, bf16[288,128]{1,0:T(8,128)(2,1)}, u32[]{:S(2)}, u32[]{:S(2)}) collective-permute-start(bf16[288,128]{1,0:T(8,128)(2,1)} %get-tuple-element.287), channel_id=1, source_target_pairs={{0,2},{1,3},{2,0},{3,1},{4,6},{5,7},{6,4},{7,5},{8,10},{9,11},{10,... | collective-permute-start | bytes 221192 | tf_op jit(solution)/shard_map/ppermute | solution.py:371
  376.5 0.8 copy-start.10
  377.3 0.6 copy-start.11
